TPU v7x, 256 devices: a whole 4x4x8 slice. The times are simulated.
256 devices in a mesh: lat: 16 (over y_hi, z), lon: 16 (over x, y_lo, core).
Axes of the slice: x: 4, y: 4 (y_hi: 2, y_lo: 2; y = y_hi * 2 + y_lo), z: 8, core: 2. Of those that a mesh axis runs over, the one named last changes fastest.
Arguments:
- query_tok: bfloat16 [256, 1024, 512], P('lat', 'lon'), may hold values from -6 to 6
- key_tok: bfloat16 [256, 1024, 512], P('lat', 'lon'), may hold values from -6 to 6
- value_tok: bfloat16 [256, 1024, 512], P('lat', 'lon'), may hold values from -6 to 6
- output_tok: bfloat16 [256, 1024, 512], P('lat', 'lon'), may hold values from -6 to 6
- grad_output: bfloat16 [256, 1024, 512], P('lat', 'lon'), may hold values from -6 to 6
- log_totals: float32 [8, 256, 1024], P(None, 'lat', 'lon'), may hold values from 2 to 4
Outputs:
- grad_query: bfloat16 [256, 1024, 512], P('lat', 'lon')
- grad_key: bfloat16 [256, 1024, 512], P('lat', 'lon')
- grad_value: bfloat16 [256, 1024, 512], P('lat', 'lon')
All inputs are finite; a program needn't handle non-finite values.
Results may differ from a plain program's by a relative error of at most 0.0053.
Values may be sent and summed in bfloat16 or wider, within the bound.
A program may use at most 64 MiB of HBM per device.

v0:
```python
import jax
import jax.numpy as jnp
from jax import lax
from jax.sharding import PartitionSpec as P


def extended(cells, sides, width, closed):
    for axis, dim in sides:
        count = lax.axis_size(axis)
        ends = count if closed else count - 1
        head = lax.slice_in_dim(cells, 0, width, axis=dim)
        tail = lax.slice_in_dim(cells, cells.shape[dim] - width, cells.shape[dim], axis=dim)
        cells = jnp.concatenate(
            [
                lax.ppermute(tail, axis, [(i, (i + 1) % count) for i in range(ends)]),
                cells,
                lax.ppermute(head, axis, [((i + 1) % count, i) for i in range(ends)]),
            ],
            axis=dim,
        )
    return cells


def shifted(array, axis, by):
    length = lax.axis_size(axis)
    return lax.ppermute(array, axis, [(i, (i + by) % length) for i in range(length)])


def shifted_2(array, axis, by):
    length = lax.axis_size(axis)
    pairs = [(i, i + by) for i in range(length) if 0 <= i + by < length]
    return lax.ppermute(array, axis, pairs)


def window_allowed(query_rows, query_cols, key_rows, key_cols, total_rows):
    first_row = jnp.clip(query_rows - 3, 0, total_rows - 7)
    row_offset = key_rows[None, :] - first_row[:, None]
    col_offset = key_cols[None, :] - query_cols[:, None] + 3
    inside = (query_rows >= 0) & (query_rows < total_rows)
    return (
        inside[:, None]
        & (row_offset >= 0)
        & (row_offset < 7)
        & (col_offset >= 0)
        & (col_offset < 7)
    )


def spread_rows(row_values, repeat_count):
    return jnp.repeat(row_values, repeat_count)


def spread_cols(col_values, tile_count):
    return jnp.tile(col_values, tile_count)


def heads_first(flat, head_count):
    return jnp.transpose(flat.reshape(flat.shape[0], head_count, -1), (1, 0, 2))


def heads_last(split):
    return jnp.transpose(split, (1, 0, 2)).reshape(split.shape[1], -1)


def block_grads(
    query_flat, grad_flat, totals, delta_flat, key_flat, value_flat, allowed, head_count, factor
):
    query_heads = heads_first(query_flat, head_count)
    grad_heads = heads_first(grad_flat, head_count)
    key_heads = heads_first(key_flat, head_count)
    value_heads = heads_first(value_flat, head_count)
    scores = (
        jnp.einsum("hqd,hkd->hqk", query_heads, key_heads, preferred_element_type=jnp.float32)
        * factor
    )
    weights = jnp.where(allowed[None], jnp.exp(scores - totals[:, :, None]), 0.0)
    prob_grad = jnp.einsum(
        "hqd,hkd->hqk", grad_heads, value_heads, preferred_element_type=jnp.float32
    )
    score_grad = (weights * (prob_grad - delta_flat[:, :, None])).astype(jnp.bfloat16)
    weights_low = weights.astype(jnp.bfloat16)
    grad_q = (
        jnp.einsum("hqk,hkd->hqd", score_grad, key_heads, preferred_element_type=jnp.float32)
        * factor
    )
    grad_k = (
        jnp.einsum("hqk,hqd->hkd", score_grad, query_heads, preferred_element_type=jnp.float32)
        * factor
    )
    grad_v = jnp.einsum("hqk,hqd->hkd", weights_low, grad_heads, preferred_element_type=jnp.float32)
    return (heads_last(grad_q), heads_last(grad_k), heads_last(grad_v))


def crop(array, starts, sizes):
    return lax.dynamic_slice(array, starts, sizes)


def per_device(query_tok, key_tok, value_tok, output_tok, grad_output, log_totals):
    band_rows, band_cols, features = query_tok.shape
    head_count = log_totals.shape[0]
    factor = (features // head_count) ** (-0.5)
    total_rows = band_rows * lax.axis_size("lat")
    first_global = lax.axis_index("lat") * band_rows
    block_rows = 4
    tile_cols = min(16, band_cols)
    blocks = band_rows // block_rows
    tiles = band_cols // tile_cols
    tile_wide = tile_cols + 6
    zero = jnp.int32(0)
    products = (grad_output.astype(jnp.float32) * output_tok.astype(jnp.float32)).reshape(
        band_rows, band_cols, head_count, -1
    )
    delta = jnp.transpose(jnp.sum(products, axis=-1), (2, 0, 1))
    key_value = jnp.stack([key_tok, value_tok])
    key_value = extended(key_value, (("lat", 1),), 3, False)
    key_value = extended(key_value, (("lon", 2),), 3, True)
    local_rows = jnp.arange(block_rows, dtype=jnp.int32)
    local_cols = jnp.arange(tile_cols, dtype=jnp.int32)
    wide_cols = jnp.arange(tile_wide, dtype=jnp.int32)

    def place(index):
        return (index // tiles * block_rows, index % tiles * tile_cols)

    def query_side(start, col_start):
        query_part = crop(
            query_tok, (start, col_start, zero), (block_rows, tile_cols, features)
        ).reshape(-1, features)
        grad_part = crop(
            grad_output, (start, col_start, zero), (block_rows, tile_cols, features)
        ).reshape(-1, features)
        totals = crop(
            log_totals, (zero, start, col_start), (head_count, block_rows, tile_cols)
        ).reshape(head_count, -1)
        delta_part = crop(
            delta, (zero, start, col_start), (head_count, block_rows, tile_cols)
        ).reshape(head_count, -1)
        region = crop(
            key_value, (zero, start, col_start, zero), (2, block_rows + 6, tile_wide, features)
        )
        key_flat = region[0].reshape(-1, features)
        value_flat = region[1].reshape(-1, features)
        query_rows = first_global + start + local_rows
        key_rows = first_global + start - 3 + jnp.arange(block_rows + 6, dtype=jnp.int32)
        allowed = window_allowed(
            spread_rows(query_rows, tile_cols),
            spread_cols(local_cols + 3, block_rows),
            spread_rows(key_rows, tile_wide),
            spread_cols(wide_cols, block_rows + 6),
            total_rows,
        )
        grad_q_part, key_part, value_part = block_grads(
            query_part,
            grad_part,
            totals,
            delta_part,
            key_flat,
            value_flat,
            allowed,
            head_count,
            factor,
        )
        grad_q_block = grad_q_part.reshape(block_rows, tile_cols, features)
        piece = jnp.stack([key_part, value_part]).reshape(2, block_rows + 6, tile_wide, features)
        return (grad_q_block, piece)

    def step(index, running):
        grad_q, partial_value = running
        start, col_start = place(index)
        query_part, piece = query_side(start, col_start)
        grad_q = lax.dynamic_update_slice(
            grad_q, query_part.astype(jnp.bfloat16), (start, col_start, zero)
        )
        corner = (zero, start, col_start, zero)
        earlier = crop(partial_value, corner, (2, block_rows + 6, tile_wide, features))
        partial_value = lax.dynamic_update_slice(partial_value, earlier + piece, corner)
        return (grad_q, partial_value)

    initial = (
        jnp.zeros_like(query_tok),
        jnp.zeros((2, band_rows + 6, band_cols + 6, features), jnp.float32),
    )
    grad_q, partial_value = lax.fori_loop(0, blocks * tiles, step, initial)
    middle = partial_value[:, :, 3 : band_cols + 3]
    for shift_by, border, target in (
        (-1, partial_value[:, :, :3], band_cols - 3),
        (1, partial_value[:, :, band_cols + 3 :], 0),
    ):
        arrived = shifted(border, "lon", shift_by)
        middle = middle.at[:, :, target : target + 3].add(arrived)
    core = middle[:, 3 : band_rows + 3]
    for shift_by, border, target in (
        (-1, middle[:, :3], band_rows - 3),
        (1, middle[:, band_rows + 3 :], 0),
    ):
        arrived = shifted_2(border, "lat", shift_by)
        core = core.at[:, target : target + 3].add(arrived)
    grad_k = core[0].astype(jnp.bfloat16)
    grad_v = core[1].astype(jnp.bfloat16)
    return (grad_q, grad_k, grad_v)


def solution(mesh):
    return jax.shard_map(
        per_device,
        mesh=mesh,
        in_specs=(
            P("lat", "lon", None),
            P("lat", "lon", None),
            P("lat", "lon", None),
            P("lat", "lon", None),
            P("lat", "lon", None),
            P(None, "lat", "lon"),
        ),
        out_specs=(P("lat", "lon", None), P("lat", "lon", None), P("lat", "lon", None)),
        check_vma=False,
    )
```

profile of v0, /device:TPU:22, one launch (start us, length us, event | category | flops | bytes accessed | tf_op | source)
XLA Modules:
  0.0 368.2 jit_solution(3107661447317889260)
XLA Ops:
  2.0 3.8 %collective-permute-start = (bf16[2,3,64,512]{3,2,1,0:T(8,128)(2,1)S(1)}, bf16[2,3,64,512]{3,2,1,0:T(8,128)(2,1)S(1)}, u32[]{:S(2)}, u32[]{:S(2)}) collective-permute-start(bf16[2,3,64,512]{3,2,1,0:T(8,128)(2,1)S(1)} %get-tuple-element.482), channel_id=1, source_target_pairs={{0,16},{16,32},{32,48},{48,64},{64,80},{80,96},{96,112},{112,128},... | collective-permute-start | bytes 1179656 | tf_op jit(solution)/shard_map/ppermute | solution.py:15
  5.8 5.6 %collective-permute-start.1 = (bf16[2,3,64,512]{3,2,1,0:T(8,128)(2,1)S(1)}, bf16[2,3,64,512]{3,2,1,0:T(8,128)(2,1)S(1)}, u32[]{:S(2)}, u32[]{:S(2)}) collective-permute-start(bf16[2,3,64,512]{3,2,1,0:T(8,128)(2,1)S(1)} %get-tuple-element.483), channel_id=1, source_target_pairs={{16,0},{32,16},{48,32},{64,48},{80,64},{96,80},{112,96},{128,112},... | collective-permute-start | bytes 1179656 | tf_op jit(solution)/shard_map/ppermute | solution.py:17
  11.5 7.2 %collective-permute-done = bf16[2,3,64,512]{3,2,1,0:T(8,128)(2,1)S(1)} collective-permute-done((bf16[2,3,64,512]{3,2,1,0:T(8,128)(2,1)S(1)}, bf16[2,3,64,512]{3,2,1,0:T(8,128)(2,1)S(1)}, u32[]{:S(2)}, u32[]{:S(2)}) %collective-permute-start) | collective-permute-done | bytes 393248 | tf_op jit(solution)/shard_map/ppermute | solution.py:15
  24.5 2.9 convert_multiply_fusion
  27.4 4.6 %reshape.374 = f32[16,64,8,64]{3,2,1,0:T(8,128)} reshape(f32[16,64,512]{2,1,0:T(8,128)} %convert_multiply_fusion) | data formatting | bytes 4194304 | tf_op jit(solution)/shard_map/reshape | solution.py:110
  31.9 3.4 reduce_sum.9
  35.5 4.1 %pad_maximum_fusion = bf16[2,22,70,512]{3,2,1,0:T(8,128)(2,1)} fusion(bf16[2,22,3,512]{3,2,1,0:T(4,128)(2,1)} %collective-permute-done.3, bf16[2,3,64,512]{3,2,1,0:T(8,128)(2,1)S(1)} %collective-permute-done.1, bf16[1,16,64,512]{3,2,1,0:T(8,128)(2,1)S(1)} %bitcast.59, bf16[1,16,64,512]{3,2,1,0:T(8,128)(2,1)S(1)} %bitcast.62, ...), kind=kLoop, calls=%fused_computation.49 | loop fusion | flops 18923520 | bytes 6307840 | tf_op jit(solution)/shard_map/concatenate | solution.py:13
  40.7 3.5 broadcast_in_dim.75
  44.2 259.6 %while.24 = (s32[]{:T(128)}, bf16[16,64,512]{2,1,0:T(8,128)(2,1)}, f32[2,22,70,512]{3,2,1,0:T(8,128)}, s32[]{:T(128)}, bf16[16,64,512]{2,1,0:T(8,128)(2,1)}, /*i...) while((s32[]{:T(128)}, bf16[16,64,512]{2,1,0:T(8,128)(2,1)}, ...), condition=%wide.region_2.3_spmd.clone.clone, body=%wide.region_1.2_spmd.clone.clone.sunk | while | flops 73661776 | bytes 15721886 | solution.py:182
  54.7 6.0 %dynamic_update_slice.30 = f32[2,22,70,512]{3,2,1,0:T(8,128)} dynamic-update-slice(f32[2,22,70,512]{3,2,1,0:T(8,128)} %get-tuple-element.574, f32[2,10,22,512]{3,2,1,0:T(8,128)S(1)} %maximum_add_fusion.2, s32[]{:T(128)} %constant.301.clone.1..sunk, s32[]{:T(128)S(6)} %select_n.126, s32[]{:T(128)S(6)} %select_n.128, s32[]{:T(128)} %constant.301.clone.1..sunk) | dynamic-update-slice | bytes 1802244 | tf_op jit(solution)/shard_map/while/body/eval_jaxpr/dynamic_update_slice | solution.py:175
  71.2 6.0 %dynamic_update_slice.30 = f32[2,22,70,512]{3,2,1,0:T(8,128)} dynamic-update-slice(f32[2,22,70,512]{3,2,1,0:T(8,128)} %get-tuple-element.574, f32[2,10,22,512]{3,2,1,0:T(8,128)S(1)} %maximum_add_fusion.2, s32[]{:T(128)} %constant.301.clone.1..sunk, s32[]{:T(128)S(6)} %select_n.126, s32[]{:T(128)S(6)} %select_n.128, s32[]{:T(128)} %constant.301.clone.1..sunk) | dynamic-update-slice | bytes 1802244 | tf_op jit(solution)/shard_map/while/body/eval_jaxpr/dynamic_update_slice | solution.py:175
  87.7 5.9 %dynamic_update_slice.30 = f32[2,22,70,512]{3,2,1,0:T(8,128)} dynamic-update-slice(f32[2,22,70,512]{3,2,1,0:T(8,128)} %get-tuple-element.574, f32[2,10,22,512]{3,2,1,0:T(8,128)S(1)} %maximum_add_fusion.2, s32[]{:T(128)} %constant.301.clone.1..sunk, s32[]{:T(128)S(6)} %select_n.126, s32[]{:T(128)S(6)} %select_n.128, s32[]{:T(128)} %constant.301.clone.1..sunk) | dynamic-update-slice | bytes 1802244 | tf_op jit(solution)/shard_map/while/body/eval_jaxpr/dynamic_update_slice | solution.py:175
  104.0 5.3 %dynamic_update_slice.30 = f32[2,22,70,512]{3,2,1,0:T(8,128)} dynamic-update-slice(f32[2,22,70,512]{3,2,1,0:T(8,128)} %get-tuple-element.574, f32[2,10,22,512]{3,2,1,0:T(8,128)S(1)} %maximum_add_fusion.2, s32[]{:T(128)} %constant.301.clone.1..sunk, s32[]{:T(128)S(6)} %select_n.126, s32[]{:T(128)S(6)} %select_n.128, s32[]{:T(128)} %constant.301.clone.1..sunk) | dynamic-update-slice | bytes 1802244 | tf_op jit(solution)/shard_map/while/body/eval_jaxpr/dynamic_update_slice | solution.py:175
  119.8 5.9 %dynamic_update_slice.30 = f32[2,22,70,512]{3,2,1,0:T(8,128)} dynamic-update-slice(f32[2,22,70,512]{3,2,1,0:T(8,128)} %get-tuple-element.574, f32[2,10,22,512]{3,2,1,0:T(8,128)S(1)} %maximum_add_fusion.2, s32[]{:T(128)} %constant.301.clone.1..sunk, s32[]{:T(128)S(6)} %select_n.126, s32[]{:T(128)S(6)} %select_n.128, s32[]{:T(128)} %constant.301.clone.1..sunk) | dynamic-update-slice | bytes 1802244 | tf_op jit(solution)/shard_map/while/body/eval_jaxpr/dynamic_update_slice | solution.py:175
  136.3 6.0 %dynamic_update_slice.30 = f32[2,22,70,512]{3,2,1,0:T(8,128)} dynamic-update-slice(f32[2,22,70,512]{3,2,1,0:T(8,128)} %get-tuple-element.574, f32[2,10,22,512]{3,2,1,0:T(8,128)S(1)} %maximum_add_fusion.2, s32[]{:T(128)} %constant.301.clone.1..sunk, s32[]{:T(128)S(6)} %select_n.126, s32[]{:T(128)S(6)} %select_n.128, s32[]{:T(128)} %constant.301.clone.1..sunk) | dynamic-update-slice | bytes 1802244 | tf_op jit(solution)/shard_map/while/body/eval_jaxpr/dynamic_update_slice | solution.py:175
  152.7 5.9 %dynamic_update_slice.30 = f32[2,22,70,512]{3,2,1,0:T(8,128)} dynamic-update-slice(f32[2,22,70,512]{3,2,1,0:T(8,128)} %get-tuple-element.574, f32[2,10,22,512]{3,2,1,0:T(8,128)S(1)} %maximum_add_fusion.2, s32[]{:T(128)} %constant.301.clone.1..sunk, s32[]{:T(128)S(6)} %select_n.126, s32[]{:T(128)S(6)} %select_n.128, s32[]{:T(128)} %constant.301.clone.1..sunk) | dynamic-update-slice | bytes 1802244 | tf_op jit(solution)/shard_map/while/body/eval_jaxpr/dynamic_update_slice | solution.py:175
  169.0 5.4 %dynamic_update_slice.30 = f32[2,22,70,512]{3,2,1,0:T(8,128)} dynamic-update-slice(f32[2,22,70,512]{3,2,1,0:T(8,128)} %get-tuple-element.574, f32[2,10,22,512]{3,2,1,0:T(8,128)S(1)} %maximum_add_fusion.2, s32[]{:T(128)} %constant.301.clone.1..sunk, s32[]{:T(128)S(6)} %select_n.126, s32[]{:T(128)S(6)} %select_n.128, s32[]{:T(128)} %constant.301.clone.1..sunk) | dynamic-update-slice | bytes 1802244 | tf_op jit(solution)/shard_map/while/body/eval_jaxpr/dynamic_update_slice | solution.py:175
  184.9 6.0 %dynamic_update_slice.30 = f32[2,22,70,512]{3,2,1,0:T(8,128)} dynamic-update-slice(f32[2,22,70,512]{3,2,1,0:T(8,128)} %get-tuple-element.574, f32[2,10,22,512]{3,2,1,0:T(8,128)S(1)} %maximum_add_fusion.2, s32[]{:T(128)} %constant.301.clone.1..sunk, s32[]{:T(128)S(6)} %select_n.126, s32[]{:T(128)S(6)} %select_n.128, s32[]{:T(128)} %constant.301.clone.1..sunk) | dynamic-update-slice | bytes 1802244 | tf_op jit(solution)/shard_map/while/body/eval_jaxpr/dynamic_update_slice | solution.py:175
  201.3 6.0 %dynamic_update_slice.30 = f32[2,22,70,512]{3,2,1,0:T(8,128)} dynamic-update-slice(f32[2,22,70,512]{3,2,1,0:T(8,128)} %get-tuple-element.574, f32[2,10,22,512]{3,2,1,0:T(8,128)S(1)} %maximum_add_fusion.2, s32[]{:T(128)} %constant.301.clone.1..sunk, s32[]{:T(128)S(6)} %select_n.126, s32[]{:T(128)S(6)} %select_n.128, s32[]{:T(128)} %constant.301.clone.1..sunk) | dynamic-update-slice | bytes 1802244 | tf_op jit(solution)/shard_map/while/body/eval_jaxpr/dynamic_update_slice | solution.py:175
  217.8 5.9 %dynamic_update_slice.30 = f32[2,22,70,512]{3,2,1,0:T(8,128)} dynamic-update-slice(f32[2,22,70,512]{3,2,1,0:T(8,128)} %get-tuple-element.574, f32[2,10,22,512]{3,2,1,0:T(8,128)S(1)} %maximum_add_fusion.2, s32[]{:T(128)} %constant.301.clone.1..sunk, s32[]{:T(128)S(6)} %select_n.126, s32[]{:T(128)S(6)} %select_n.128, s32[]{:T(128)} %constant.301.clone.1..sunk) | dynamic-update-slice | bytes 1802244 | tf_op jit(solution)/shard_map/while/body/eval_jaxpr/dynamic_update_slice | solution.py:175
  234.0 5.3 %dynamic_update_slice.30 = f32[2,22,70,512]{3,2,1,0:T(8,128)} dynamic-update-slice(f32[2,22,70,512]{3,2,1,0:T(8,128)} %get-tuple-element.574, f32[2,10,22,512]{3,2,1,0:T(8,128)S(1)} %maximum_add_fusion.2, s32[]{:T(128)} %constant.301.clone.1..sunk, s32[]{:T(128)S(6)} %select_n.126, s32[]{:T(128)S(6)} %select_n.128, s32[]{:T(128)} %constant.301.clone.1..sunk) | dynamic-update-slice | bytes 1802244 | tf_op jit(solution)/shard_map/while/body/eval_jaxpr/dynamic_update_slice | solution.py:175
  249.9 5.9 %dynamic_update_slice.30 = f32[2,22,70,512]{3,2,1,0:T(8,128)} dynamic-update-slice(f32[2,22,70,512]{3,2,1,0:T(8,128)} %get-tuple-element.574, f32[2,10,22,512]{3,2,1,0:T(8,128)S(1)} %maximum_add_fusion.2, s32[]{:T(128)} %constant.301.clone.1..sunk, s32[]{:T(128)S(6)} %select_n.126, s32[]{:T(128)S(6)} %select_n.128, s32[]{:T(128)} %constant.301.clone.1..sunk) | dynamic-update-slice | bytes 1802244 | tf_op jit(solution)/shard_map/while/body/eval_jaxpr/dynamic_update_slice | solution.py:175
  266.2 5.8 %dynamic_update_slice.30 = f32[2,22,70,512]{3,2,1,0:T(8,128)} dynamic-update-slice(f32[2,22,70,512]{3,2,1,0:T(8,128)} %get-tuple-element.574, f32[2,10,22,512]{3,2,1,0:T(8,128)S(1)} %maximum_add_fusion.2, s32[]{:T(128)} %constant.301.clone.1..sunk, s32[]{:T(128)S(6)} %select_n.126, s32[]{:T(128)S(6)} %select_n.128, s32[]{:T(128)} %constant.301.clone.1..sunk) | dynamic-update-slice | bytes 1802244 | tf_op jit(solution)/shard_map/while/body/eval_jaxpr/dynamic_update_slice | solution.py:175
  282.5 5.8 %dynamic_update_slice.30 = f32[2,22,70,512]{3,2,1,0:T(8,128)} dynamic-update-slice(f32[2,22,70,512]{3,2,1,0:T(8,128)} %get-tuple-element.574, f32[2,10,22,512]{3,2,1,0:T(8,128)S(1)} %maximum_add_fusion.2, s32[]{:T(128)} %constant.301.clone.1..sunk, s32[]{:T(128)S(6)} %select_n.126, s32[]{:T(128)S(6)} %select_n.128, s32[]{:T(128)} %constant.301.clone.1..sunk) | dynamic-update-slice | bytes 1802244 | tf_op jit(solution)/shard_map/while/body/eval_jaxpr/dynamic_update_slice | solution.py:175
  298.7 5.2 %dynamic_update_slice.30 = f32[2,22,70,512]{3,2,1,0:T(8,128)} dynamic-update-slice(f32[2,22,70,512]{3,2,1,0:T(8,128)} %get-tuple-element.574, f32[2,10,22,512]{3,2,1,0:T(8,128)S(1)} %maximum_add_fusion.2, s32[]{:T(128)} %constant.301.clone.1..sunk, s32[]{:T(128)S(6)} %select_n.126, s32[]{:T(128)S(6)} %select_n.128, s32[]{:T(128)} %constant.301.clone.1..sunk) | dynamic-update-slice | bytes 1802244 | tf_op jit(solution)/shard_map/while/body/eval_jaxpr/dynamic_update_slice | solution.py:175
  305.1 4.9 %collective-permute-done.4 = f32[2,22,3,512]{3,2,1,0:T(4,128)S(1)} collective-permute-done((f32[2,22,3,512]{3,2,1,0:T(4,128)S(1)}, f32[2,22,3,512]{3,2,1,0:T(4,128)S(1)}, u32[]{:S(2)}, u32[]{:S(2)}) %collective-permute-start.4) | collective-permute-done | bytes 270368 | tf_op jit(solution)/shard_map/ppermute | solution.py:26
  313.4 6.4 %slice.182 = f32[2,22,64,512]{3,2,1,0:T(8,128)} slice(f32[2,22,70,512]{3,2,1,0:T(8,128)} %get-tuple-element.387), slice={[0:2], [0:22], [3:67], [0:512]} | slice | bytes 11534336 | tf_op jit(solution)/shard_map/slice | solution.py:183
  319.8 5.4 %scatter-add.14 = f32[2,22,64,512]{3,2,1,0:T(8,128)} dynamic-update-slice(f32[2,22,64,512]{3,2,1,0:T(8,128)} %slice.182, f32[2,22,3,512]{3,2,1,0:T(4,128)S(1)} %get-tuple-element.475, s32[]{:T(128)} %constant.301.clone.1, s32[]{:T(128)} %constant.301.clone.1, s32[]{:T(128)} %constant.307.clone.1, s32[]{:T(128)} %constant.301.clone.1) | dynamic-update-slice | bytes 540676 | tf_op jit(solution)/shard_map/scatter-add | solution.py:189
  326.4 6.1 %scatter-add.15 = f32[2,22,64,512]{3,2,1,0:T(8,128)} dynamic-update-slice(f32[2,22,64,512]{3,2,1,0:T(8,128)} %scatter-add.14, f32[2,22,3,512]{3,2,1,0:T(4,128)S(1)} %slice_add_fusion.2, s32[]{:T(128)} %constant.301.clone.1, s32[]{:T(128)} %constant.301.clone.1, s32[]{:T(128)} %constant.301.clone.1, s32[]{:T(128)} %constant.301.clone.1) | dynamic-update-slice | bytes 540676 | tf_op jit(solution)/shard_map/scatter-add | solution.py:189
  334.1 7.4 %collective-permute-start.6 = (f32[2,3,64,512]{3,2,1,0:T(8,128)S(1)}, f32[2,3,64,512]{3,2,1,0:T(8,128)S(1)}, u32[]{:S(2)}, u32[]{:S(2)}) collective-permute-start(f32[2,3,64,512]{3,2,1,0:T(8,128)S(1)} %get-tuple-element.477), channel_id=1, source_target_pairs={{16,0},{32,16},{48,32},{64,48},{80,64},{96,80},{112,96},{128,112},... | collective-permute-start | bytes 2359304 | tf_op jit(solution)/shard_map/ppermute | solution.py:32
  346.2 12.3 %collective-permute-done.6 = f32[2,3,64,512]{3,2,1,0:T(8,128)S(1)} collective-permute-done((f32[2,3,64,512]{3,2,1,0:T(8,128)S(1)}, f32[2,3,64,512]{3,2,1,0:T(8,128)S(1)}, u32[]{:S(2)}, u32[]{:S(2)}) %collective-permute-start.6) | collective-permute-done | bytes 786464 | tf_op jit(solution)/shard_map/ppermute | solution.py:32
  359.8 6.5 %collective-permute-done.7 = f32[2,3,64,512]{3,2,1,0:T(8,128)S(1)} collective-permute-done((f32[2,3,64,512]{3,2,1,0:T(8,128)S(1)}, f32[2,3,64,512]{3,2,1,0:T(8,128)S(1)}, u32[]{:S(2)}, u32[]{:S(2)}) %collective-permute-start.7) | collective-permute-done | bytes 786464 | tf_op jit(solution)/shard_map/ppermute | solution.py:32
  (652 shorter events, 189.3 us)
Async XLA Ops:
  0.6 23.8 %copy-start.2 = (bf16[16,64,512]{2,1,0:T(8,128)(2,1)S(1)}, bf16[16,64,512]{2,1,0:T(8,128)(2,1)}, u32[]{:S(2)}) copy-start(bf16[16,64,512]{2,1,0:T(8,128)(2,1)} %param.19) | copy-start | bytes 3145732
  2.0 16.6 %collective-permute-start = (bf16[2,3,64,512]{3,2,1,0:T(8,128)(2,1)S(1)}, bf16[2,3,64,512]{3,2,1,0:T(8,128)(2,1)S(1)}, u32[]{:S(2)}, u32[]{:S(2)}) collective-permute-start(bf16[2,3,64,512]{3,2,1,0:T(8,128)(2,1)S(1)} %get-tuple-element.482), channel_id=1, source_target_pairs={{0,16},{16,32},{32,48},{48,64},{64,80},{80,96},{96,112},{112,128},... | collective-permute-start | bytes 1179656 | tf_op jit(solution)/shard_map/ppermute | solution.py:15
  5.8 14.0 %collective-permute-start.1 = (bf16[2,3,64,512]{3,2,1,0:T(8,128)(2,1)S(1)}, bf16[2,3,64,512]{3,2,1,0:T(8,128)(2,1)S(1)}, u32[]{:S(2)}, u32[]{:S(2)}) collective-permute-start(bf16[2,3,64,512]{3,2,1,0:T(8,128)(2,1)S(1)} %get-tuple-element.483), channel_id=1, source_target_pairs={{16,0},{32,16},{48,32},{64,48},{80,64},{96,80},{112,96},{128,112},... | collective-permute-start | bytes 1179656 | tf_op jit(solution)/shard_map/ppermute | solution.py:17
  21.8 13.7 %collective-permute-start.2 = (bf16[2,22,3,512]{3,2,1,0:T(4,128)(2,1)}, bf16[2,22,3,512]{3,2,1,0:T(4,128)(2,1)}, u32[]{:S(2)}, u32[]{:S(2)}) collective-permute-start(bf16[2,22,3,512]{3,2,1,0:T(4,128)(2,1)} %get-tuple-element.478), channel_id=1, source_target_pairs={{0,1},{1,2},{2,3},{3,4},{4,5},{5,6},{6,7},{7,8},{8,9},{9,10},{10,1... | collective-permute-start | bytes 405512 | tf_op jit(solution)/shard_map/ppermute | solution.py:15
  21.8 13.7 %collective-permute-start.3 = (bf16[2,22,3,512]{3,2,1,0:T(4,128)(2,1)}, bf16[2,22,3,512]{3,2,1,0:T(4,128)(2,1)}, u32[]{:S(2)}, u32[]{:S(2)}) collective-permute-start(bf16[2,22,3,512]{3,2,1,0:T(4,128)(2,1)} %get-tuple-element.479), channel_id=1, source_target_pairs={{1,0},{2,1},{3,2},{4,3},{5,4},{6,5},{7,6},{8,7},{9,8},{10,9},{11,1... | collective-permute-start | bytes 405512 | tf_op jit(solution)/shard_map/ppermute | solution.py:17
  27.3 8.1 %copy-start = (bf16[16,64,512]{2,1,0:T(8,128)(2,1)S(1)}, bf16[16,64,512]{2,1,0:T(8,128)(2,1)}, u32[]{:S(2)}) copy-start(bf16[16,64,512]{2,1,0:T(8,128)(2,1)} %param.18) | copy-start | bytes 3145732
  27.3 8.2 %copy-start.1 = (bf16[16,64,512]{2,1,0:T(8,128)(2,1)S(1)}, bf16[16,64,512]{2,1,0:T(8,128)(2,1)}, u32[]{:S(2)}) copy-start(bf16[16,64,512]{2,1,0:T(8,128)(2,1)} %param.17) | copy-start | bytes 3145732
  305.0 5.0 %collective-permute-start.4 = (f32[2,22,3,512]{3,2,1,0:T(4,128)S(1)}, f32[2,22,3,512]{3,2,1,0:T(4,128)S(1)}, u32[]{:S(2)}, u32[]{:S(2)}) collective-permute-start(f32[2,22,3,512]{3,2,1,0:T(4,128)S(1)} %slice.184), channel_id=1, source_target_pairs={{0,15},{1,0},{2,1},{3,2},{4,3},{5,4},{6,5},{7,6},{8,7},{9,8},{10,9... | collective-permute-start | bytes 811016 | tf_op jit(solution)/shard_map/ppermute | solution.py:26
  311.6 13.6 %collective-permute-start.5 = (f32[2,22,3,512]{3,2,1,0:T(4,128)S(1)}, f32[2,22,3,512]{3,2,1,0:T(4,128)S(1)}, u32[]{:S(2)}, u32[]{:S(2)}) collective-permute-start(f32[2,22,3,512]{3,2,1,0:T(4,128)S(1)} %get-tuple-element.474), channel_id=1, source_target_pairs={{0,1},{1,2},{2,3},{3,4},{4,5},{5,6},{6,7},{7,8},{8,9},{9,10},{10,1... | collective-permute-start | bytes 811016 | tf_op jit(solution)/shard_map/ppermute | solution.py:26
  334.1 24.4 %collective-permute-start.6 = (f32[2,3,64,512]{3,2,1,0:T(8,128)S(1)}, f32[2,3,64,512]{3,2,1,0:T(8,128)S(1)}, u32[]{:S(2)}, u32[]{:S(2)}) collective-permute-start(f32[2,3,64,512]{3,2,1,0:T(8,128)S(1)} %get-tuple-element.477), channel_id=1, source_target_pairs={{16,0},{32,16},{48,32},{64,48},{80,64},{96,80},{112,96},{128,112},... | collective-permute-start | bytes 2359304 | tf_op jit(solution)/shard_map/ppermute | solution.py:32
  341.5 24.7 %collective-permute-start.7 = (f32[2,3,64,512]{3,2,1,0:T(8,128)S(1)}, f32[2,3,64,512]{3,2,1,0:T(8,128)S(1)}, u32[]{:S(2)}, u32[]{:S(2)}) collective-permute-start(f32[2,3,64,512]{3,2,1,0:T(8,128)S(1)} %get-tuple-element.476), channel_id=1, source_target_pairs={{0,16},{16,32},{32,48},{48,64},{64,80},{80,96},{96,112},{112,128},... | collective-permute-start | bytes 2359304 | tf_op jit(solution)/shard_map/ppermute | solution.py:32
where the time goes:
time: 376 us; the launch traced here: 368 us
  local copies, waits for them, and re-layouts  245 us (65%)
  other arithmetic  45.6 us (12%)
  waiting for transfers between devices  32 us (9%)
  starting transfers between devices  23.3 us (6%)
  matrix products  19.5 us (5%)
    dynamic_update_slice x16, local copies, waits for them, and re-layouts, step(): lax.dynamic_update_slice(partial_value, earlier + piece, corner)  92.2 us
    dynamic_slice x32, local copies, waits for them, and re-layouts, crop(): return lax.dynamic_slice(array, starts, sizes)  27.8 us
    add x16, other arithmetic, step(): earlier + piece  25.1 us
    slice x16, local copies, waits for them, and re-layouts, query_side(): value_flat = region[1].reshape(-1, features)  19.8 us
    ppermute x2, waiting for transfers between devices, shifted_2(): return lax.ppermute(array, axis, pairs)  18.7 us
    squeeze x64, local copies, waits for them, and re-layouts, heads_first(): return jnp.transpose(flat.reshape(flat.shape[0], head_count, -1), (1, 0, 2))  18.2 us
    scatter-add x2, local copies, waits for them, and re-layouts, per_device(): middle = middle.at[:, :, target:target + 3].add(arrived)  11.5 us
    dynamic_update_slice x16, local copies, waits for them, and re-layouts, step(): lax.dynamic_update_slice(grad_q, query_part.astype(jnp.bfloat16), (start,...  10.3 us
  transfers between devices with their start and end apart: 8, of which 5 were waited for; matrix products, arithmetic and copies ran while one was open for 7% of the time, Pallas kernels for 0%

commit v1 on v0

v1 whole, which is shorter than its diff:
```python
import functools

import jax
import jax.numpy as jnp
from jax import lax
from jax.experimental import pallas as pl
from jax.experimental.pallas import tpu as pltpu
from jax.sharding import PartitionSpec as P

MESH = pl.DeviceIdType.MESH
BF = jnp.bfloat16
F32 = jnp.float32
BIG = 32768.0
EXP_SCALE = 0.125 * 1.4426950408889634
CHUNKS = 2


def _iota(shape, dim):
    return lax.broadcasted_iota(jnp.int32, shape, dim)


def _dot(a, b, dims):
    return lax.dot_general(a, b, (dims, ((), ())), preferred_element_type=F32)


def _keep(mask, x):
    return jnp.where(mask, x, jnp.zeros_like(x))


def _flat(x):
    return x.reshape(-1, x.shape[-1])


def _key_features(base, row0, rows, q_base, total):
    shape = (2 * rows * 8, 128)
    key = _iota(shape, 0)
    lane = _iota(shape, 1)
    tile = key // (rows * 8)
    k_row = base + row0 + key // 8 % rows
    k_col = tile * 8 + key % 8
    group, slot = lane // 16, lane % 16
    q_row = q_base + 2 * group + slot - 6
    first = jnp.clip(q_row - 3, 0, total - 7)
    row_ok = (k_row >= first) & (k_row < first + 7)
    gap = k_col - 4 - group
    col_ok = (gap >= -3) & (gap <= 3)
    row_slot = (slot == 6) | (slot == 7)
    bad = (row_slot & jnp.logical_not(row_ok)) | ((slot == 8) & jnp.logical_not(col_ok))
    value = jnp.where(bad, -BIG, jnp.where(slot < 3, -8.0, 0.0))
    return value.astype(BF)


def _prob_features(keys):
    slot = _iota((keys, 128), 1) % 16
    return jnp.where((slot >= 3) & (slot < 6), -1.0, 0.0).astype(BF)


def _split3(x):
    a = x.astype(BF).astype(F32)
    rest = x - a
    b = rest.astype(BF).astype(F32)
    return a, b, rest - b


def kernel(
    n_lat,
    n_lon,
    q_hbm,
    k_hbm,
    v_hbm,
    o_hbm,
    g_hbm,
    lt_hbm,
    dq_out,
    dk_out,
    dv_out,
    qv,
    kv,
    vv,
    ov,
    gv,
    ltv,
    aug,
    ksh,
    vsh,
    dq_acc,
    dk_acc,
    dv_acc,
    feat,
    feat_halo,
    rim_in,
    q_halo,
    g_halo,
    a_halo,
    dq_send,
    dq_recv,
    rim_send,
    rim_recv,
    load_sem,
    rim_sems,
    row_sems,
    back_sems,
    grad_sems,
):
    lat = lax.axis_index("lat")
    lon = lax.axis_index("lon")
    left = (lat, lax.rem(lon + n_lon - 1, n_lon))
    right = (lat, lax.rem(lon + 1, n_lon))
    above = (lat - 1, lon)
    below = (lat + 1, lon)
    has_above = lat > 0
    has_below = lat < n_lat - 1
    total = n_lat * 16
    base = lat * 16
    width = 8 // CHUNKS

    loads = [
        pltpu.make_async_copy(src, dst, load_sem.at[i])
        for i, (src, dst) in enumerate(
            ((g_hbm, gv), (o_hbm, ov), (lt_hbm, ltv), (k_hbm, kv), (v_hbm, vv), (q_hbm, qv))
        )
    ]
    for load in loads:
        load.start()

    barrier = pltpu.get_barrier_semaphore()

    def greet(device):
        pl.semaphore_signal(barrier, inc=1, device_id=device, device_id_type=MESH)

    greet(left)
    greet(right)
    pl.when(has_above)(lambda: greet(above))
    pl.when(has_below)(lambda: greet(below))
    peers = 2 + jnp.minimum(lat, 1) + jnp.minimum(n_lat - 1 - lat, 1)
    pl.semaphore_wait(barrier, peers)

    def remote(src, dst, sems, index, device):
        return pltpu.make_async_remote_copy(
            src_ref=src,
            dst_ref=dst,
            send_sem=sems.at[(0,) + index],
            recv_sem=sems.at[(1,) + index],
            device_id=device,
            device_id_type=MESH,
        )

    def row_copy(what, chunk, side):
        src, dst = ((q_hbm, q_halo), (g_hbm, g_halo), (aug, a_halo))[what]
        rows = pl.ds(13, 3) if side == 0 else pl.ds(0, 3)
        strips = pl.ds(chunk * width, width)
        return remote(
            src.at[rows, strips],
            dst.at[side, pl.ds(0, 3), strips],
            row_sems,
            (what, chunk, side),
            below if side == 0 else above,
        )

    def rim_copy(what, side):
        src = (k_hbm, v_hbm)[what]
        return remote(
            src.at[:, 7 if side == 0 else 0],
            rim_in.at[side, what],
            rim_sems,
            (what, side),
            right if side == 0 else left,
        )

    def back_copy(chunk, side):
        strips = pl.ds(chunk * width, width)
        return remote(
            dq_send.at[side, :, strips],
            dq_recv.at[1 - side, :, strips],
            back_sems,
            (chunk, 1 - side),
            above if side == 0 else below,
        )

    def grad_copy(what, side):
        return remote(
            rim_send.at[side, what],
            rim_recv.at[side, what],
            grad_sems,
            (what, side),
            right if side == 0 else left,
        )

    def send_rows(whats, side):
        for chunk in range(CHUNKS):
            for what in whats:
                row_copy(what, chunk, side).start()

    pl.when(has_below)(lambda: send_rows((0, 1), 0))
    pl.when(has_above)(lambda: send_rows((0, 1), 1))
    for what in range(2):
        for side in range(2):
            rim_copy(what, side).start()

    slot16 = _iota((1, 128), 1) % 16
    group16 = _iota((1, 128), 1) // 16
    low = _iota((1, 128), 1) < 64
    head_keep = [(group16 == h) | (slot16 >= 6) for h in range(8)]
    for t in range(2):
        feat[t] = _key_features(base, 8 * t, 8, base, total)
    feat_halo[0] = _key_features(base, 0, 4, base - 16, total)
    feat_halo[1] = _key_features(base, 12, 4, base + 16, total)

    @pl.loop(0, 9)
    def _(tile):
        dk_acc[tile] = jnp.zeros((16, 8, 512), F32)
        dv_acc[tile] = jnp.zeros((16, 8, 512), F32)

    for side in range(2):
        q_halo[side, 3] = jnp.zeros((8, 8, 512), BF)
        g_halo[side, 3] = jnp.zeros((8, 8, 512), BF)
        a_halo[side, 3] = jnp.zeros((8, 8, 128), BF)

    feature = _iota((512, 128), 0)
    lane = _iota((512, 128), 1)
    spread = jnp.where(
        (lane // 16 == feature // 64) & (lane % 16 >= 3) & (lane % 16 < 6), 1.0, 0.0
    ).astype(BF)
    for load in loads[:3]:
        load.wait()
    parts = _split3(ltv[...].T)
    column = _iota((64, 128), 0) % 8
    group = _iota((64, 128), 1) // 16
    slot = _iota((64, 128), 1) % 16
    col_hot = jnp.where((slot == 8) & (group == column), 1.0, 0.0)

    def features_of(r):
        product = _flat(gv[r].astype(F32)) * _flat(ov[r].astype(F32))
        high = product.astype(BF)
        rest = (product - high.astype(F32)).astype(BF)
        delta = _dot(high, spread, ((1,), (0,))) + _dot(rest, spread, ((1,), (0,)))
        d0, d1, d2 = _split3(delta)
        rolled = [pltpu.roll(part, (i - r) % 128, 1) for i, part in enumerate(parts)]
        value = jnp.where((slot >= 6) & (slot < 8) & (2 * group + slot - 6 == r), 1.0, col_hot)
        for i, x in enumerate(rolled + [d0, d1, d2]):
            value = jnp.where(slot == i, x, value)
        aug[r] = value.astype(BF).reshape(8, 8, 128)

    for r in (13, 14, 15):
        features_of(r)
    pl.when(has_below)(lambda: send_rows((2,), 0))
    for r in (0, 1, 2):
        features_of(r)
    pl.when(has_above)(lambda: send_rows((2,), 1))
    for r in range(3, 13):
        features_of(r)

    half = _iota((1, 8, 512), 1) < 4

    def turned(x):
        return pltpu.roll(x.astype(F32), 4, 1)

    for load in loads[3:5]:
        load.wait()

    @pl.loop(1, 8)
    def _(tile):
        for src, dst in ((kv, ksh), (vv, vsh)):
            dst[tile] = jnp.where(half, turned(src[:, tile - 1]), turned(src[:, tile])).astype(BF)

    loads[5].wait()
    prob_feat = _prob_features(128)

    def two(x):
        return jnp.concatenate([_keep(low, x), _keep(jnp.logical_not(low), x)], axis=0)

    def unit(s, t, p):
        lanes = pl.ds(128 * p, 128)
        k_rows = pl.ds(8 * t, 8)
        q_rows = pl.ds(4 * t, 12)
        keys = jnp.concatenate(
            [_flat(ksh[s, k_rows, :, lanes]), _flat(ksh[s + 1, k_rows, :, lanes])], axis=0
        )
        values = jnp.concatenate(
            [_flat(vsh[s, k_rows, :, lanes]), _flat(vsh[s + 1, k_rows, :, lanes])], axis=0
        )
        q2 = two(_flat(qv[q_rows, s, :, lanes]))
        g2 = two(_flat(gv[q_rows, s, :, lanes]))
        extra = _flat(aug[q_rows, s])
        a2 = jnp.concatenate(
            [_keep(head_keep[2 * p], extra), _keep(head_keep[2 * p + 1], extra)], axis=0
        )
        scores = _dot(
            jnp.concatenate([keys, feat[t]], axis=1),
            jnp.concatenate([q2, a2], axis=1),
            ((1,), (1,)),
        )
        prob_grad = _dot(
            jnp.concatenate([values, prob_feat], axis=1),
            jnp.concatenate([g2, a2], axis=1),
            ((1,), (1,)),
        )
        weights = jnp.exp2(scores * EXP_SCALE)
        score_grad = (weights * prob_grad).astype(BF)
        d_keys = _dot(score_grad, q2, ((1,), (0,)))
        d_values = _dot(weights.astype(BF), g2, ((1,), (0,)))
        turned_grad = score_grad.T
        d_query = _dot(
            jnp.concatenate([turned_grad[:96], turned_grad[96:]], axis=1),
            two(keys),
            ((1,), (0,)),
        )
        for acc, d in ((dk_acc, d_keys), (dv_acc, d_values)):
            acc[s, k_rows, :, lanes] += d[:64].reshape(8, 8, 128)
            acc[s + 1, k_rows, :, lanes] += d[64:].reshape(8, 8, 128)
        return d_query

    def strip(s):
        for p in range(4):
            lanes = pl.ds(128 * p, 128)
            upper = unit(s, 0, p)
            lower = unit(s, 1, p)
            dq_acc[pl.ds(0, 4), s, :, lanes] = upper[:32].reshape(4, 8, 128)
            dq_acc[pl.ds(4, 8), s, :, lanes] = (upper[32:] + lower[:64]).reshape(8, 8, 128)
            dq_acc[pl.ds(12, 4), s, :, lanes] = lower[64:].reshape(4, 8, 128)

    @pl.loop(1, 7)
    def _(s):
        strip(s)

    for what in range(2):
        for side in range(2):
            rim_copy(what, side).wait()
    for i, (src, dst) in enumerate(((kv, ksh), (vv, vsh))):
        dst[0] = jnp.where(half, turned(rim_in[0, i]), turned(src[:, 0])).astype(BF)
        dst[8] = jnp.where(half, turned(src[:, 7]), turned(rim_in[1, i])).astype(BF)

    @pl.loop(0, 2)
    def _(i):
        strip(7 * i)

    lane512 = _iota((1, 512), 1)
    prob_halo = _prob_features(64)

    def halo_unit(s, side):
        rows = pl.ds(12 * side, 4)
        keys = jnp.concatenate([_flat(ksh[s, rows]), _flat(ksh[s + 1, rows])], axis=0)
        values = jnp.concatenate([_flat(vsh[s, rows]), _flat(vsh[s + 1, rows])], axis=0)
        q = _flat(q_halo[side, :, s])
        g = _flat(g_halo[side, :, s])
        extra = _flat(a_halo[side, :, s])
        q8 = jnp.concatenate([_keep(lane512 // 64 == h, q) for h in range(8)], axis=0)
        g8 = jnp.concatenate([_keep(lane512 // 64 == h, g) for h in range(8)], axis=0)
        a8 = jnp.concatenate([_keep(head_keep[h], extra) for h in range(8)], axis=0)
        scores = _dot(
            jnp.concatenate([keys, feat_halo[side]], axis=1),
            jnp.concatenate([q8, a8], axis=1),
            ((1,), (1,)),
        )
        prob_grad = _dot(
            jnp.concatenate([values, prob_halo], axis=1),
            jnp.concatenate([g8, a8], axis=1),
            ((1,), (1,)),
        )
        weights = jnp.exp2(scores * EXP_SCALE)
        score_grad = (weights * prob_grad).astype(BF)
        d_keys = _dot(score_grad, q8, ((1,), (0,)))
        d_values = _dot(weights.astype(BF), g8, ((1,), (0,)))
        turned_grad = score_grad.T
        for p in range(4):
            lanes = slice(128 * p, 128 * p + 128)
            d_query = _dot(turned_grad[64 * p : 64 * p + 64], keys[:, lanes], ((1,), (0,)))
            d_query = jnp.where(low, d_query[:32], d_query[32:]) * 0.125
            dq_send[side, :, s, :, lanes] = d_query[:24].reshape(3, 8, 128).astype(BF)
        for acc, d in ((dk_acc, d_keys), (dv_acc, d_values)):
            acc[s, rows] += d[:32].reshape(4, 8, 512)
            acc[s + 1, rows] += d[32:].reshape(4, 8, 512)

    def halo(chunk, side):
        for what in range(3):
            row_copy(what, chunk, side).wait_recv()

        @pl.loop(chunk * width, (chunk + 1) * width)
        def _(s):
            halo_unit(s, side)

        back_copy(chunk, side).start()

    for chunk in range(CHUNKS):
        pl.when(has_above)(functools.partial(halo, chunk, 0))
        pl.when(has_below)(functools.partial(halo, chunk, 1))

    half8 = _iota((1, 8, 512), 1) < 4
    for what, acc in enumerate((dk_acc, dv_acc)):
        scale = 0.125 if what == 0 else 1.0
        for i in range(8):
            a, b = acc[8, 2 * i], acc[8, 2 * i + 1]
            rim_send[0, what, i] = (
                jnp.where(half8[0], pltpu.roll(a, 4, 0), b) * scale
            ).astype(BF)
            a, b = acc[0, 2 * i], acc[0, 2 * i + 1]
            rim_send[1, what, i] = (
                jnp.where(half8[0], a, pltpu.roll(b, 4, 0)) * scale
            ).astype(BF)
        for side in range(2):
            grad_copy(what, side).start()

    @pl.loop(3, 13)
    def _(r):
        dq_out[r] = (dq_acc[r] * 0.125).astype(BF)

    def merged(acc, j, scale):
        return pltpu.roll(jnp.where(half, acc[j + 1], acc[j]), 4, 1) * scale

    @pl.loop(1, 7)
    def _(j):
        dk_out[:, j] = merged(dk_acc, j, 0.125).astype(BF)
        dv_out[:, j] = merged(dv_acc, j, 1.0).astype(BF)

    for what in range(2):
        for side in range(2):
            grad_copy(what, side).wait()
    for what, (acc, out) in enumerate(((dk_acc, dk_out), (dv_acc, dv_out))):
        scale = 0.125 if what == 0 else 1.0
        edge = merged(acc, 0, scale)
        came = rim_recv[0, what].astype(F32)
        spun = pltpu.roll(came, 4, 1)
        for i in range(8):
            out[2 * i, 0] = (edge[2 * i] + _keep(half8[0], came[i])).astype(BF)
            out[2 * i + 1, 0] = (edge[2 * i + 1] + _keep(half8[0], spun[i])).astype(BF)
        edge = merged(acc, 7, scale)
        came = rim_recv[1, what].astype(F32)
        spun = pltpu.roll(came, 4, 1)
        for i in range(8):
            out[2 * i, 7] = (edge[2 * i] + _keep(jnp.logical_not(half8[0]), spun[i])).astype(BF)
            out[2 * i + 1, 7] = (
                edge[2 * i + 1] + _keep(jnp.logical_not(half8[0]), came[i])
            ).astype(BF)

    def finish(side, rows):
        @pl.when(has_above if side == 0 else has_below)
        def _():
            for chunk in range(CHUNKS):
                back_copy(chunk, 1 - side).wait_recv()
            for r in range(3):
                dq_out[rows + r] = (
                    dq_acc[rows + r] * 0.125 + dq_recv[side, r].astype(F32)
                ).astype(BF)

        @pl.when(jnp.logical_not(has_above if side == 0 else has_below))
        def _():
            for r in range(3):
                dq_out[rows + r] = (dq_acc[rows + r] * 0.125).astype(BF)

    finish(0, 0)
    finish(1, 13)

    def drain(send_side, back_side):
        for chunk in range(CHUNKS):
            for what in range(3):
                row_copy(what, chunk, send_side).wait_send()
            back_copy(chunk, back_side).wait_send()

    pl.when(has_below)(lambda: drain(0, 1))
    pl.when(has_above)(lambda: drain(1, 0))


def solution(mesh):
    n_lat, n_lon = mesh.shape["lat"], mesh.shape["lon"]

    def per_device(query_tok, key_tok, value_tok, output_tok, grad_output, log_totals):
        def tiled(x):
            return x.reshape(16, 8, 8, 512)

        dma = pltpu.SemaphoreType.DMA
        token = (16, 8, 8, 512)
        shifted = (9, 16, 8, 512)
        outs = pl.pallas_call(
            functools.partial(kernel, n_lat, n_lon),
            out_shape=[jax.ShapeDtypeStruct(token, BF)] * 3,
            in_specs=[pl.BlockSpec(memory_space=pl.ANY)] * 6,
            out_specs=[pl.BlockSpec(memory_space=pltpu.VMEM)] * 3,
            scratch_shapes=[
                pltpu.VMEM(token, BF),
                pltpu.VMEM(token, BF),
                pltpu.VMEM(token, BF),
                pltpu.VMEM(token, BF),
                pltpu.VMEM(token, BF),
                pltpu.VMEM((128, 64), F32),
                pltpu.VMEM((16, 8, 8, 128), BF),
                pltpu.VMEM(shifted, BF),
                pltpu.VMEM(shifted, BF),
                pltpu.VMEM(token, F32),
                pltpu.VMEM(shifted, F32),
                pltpu.VMEM(shifted, F32),
                pltpu.VMEM((2, 128, 128), BF),
                pltpu.VMEM((2, 64, 128), BF),
                pltpu.VMEM((2, 2, 16, 8, 512), BF),
                pltpu.VMEM((2, 4, 8, 8, 512), BF),
                pltpu.VMEM((2, 4, 8, 8, 512), BF),
                pltpu.VMEM((2, 4, 8, 8, 128), BF),
                pltpu.VMEM((2, 3, 8, 8, 512), BF),
                pltpu.VMEM((2, 3, 8, 8, 512), BF),
                pltpu.VMEM((2, 2, 8, 8, 512), BF),
                pltpu.VMEM((2, 2, 8, 8, 512), BF),
                dma((6,)),
                dma((2, 2, 2)),
                dma((2, 3, CHUNKS, 2)),
                dma((2, CHUNKS, 2)),
                dma((2, 2, 2)),
            ],
            compiler_params=pltpu.CompilerParams(
                collective_id=0,
                has_side_effects=True,
                vmem_limit_bytes=56 * 1024 * 1024,
            ),
        )(
            tiled(query_tok),
            tiled(key_tok),
            tiled(value_tok),
            tiled(output_tok),
            tiled(grad_output),
            log_totals.reshape(128, 64),
        )
        return tuple(x.reshape(16, 64, 512) for x in outs)

    return jax.shard_map(
        per_device,
        mesh=mesh,
        in_specs=(P("lat", "lon", None),) * 5 + (P(None, "lat", "lon"),),
        out_specs=(P("lat", "lon", None),) * 3,
        check_vma=False,
    )
```

time: 376 us -> 49.8 us (0.13)
  the two profiles are of different devices: /device:TPU:22 before, /device:TPU:17 now
where the time goes in v1:
time: 49.8 us; the launch traced here: 49.7 us
  Pallas kernels  44.1 us (89%)
  local copies, waits for them, and re-layouts  4.95 us (10%)
  between operations  0.65 us (1%)
    pallas_call x1, Pallas kernels, per_device(): pl.pallas_call(functools.partial(kernel, n_lat, n_lon), out_shape=[jax.Sh...  44.1 us
    unnamed x7, local copies, waits for them, and re-layouts  4.95 us

profile of v1, /device:TPU:17, one launch (start us, length us, event | category | flops | bytes accessed | tf_op | source)
XLA Modules:
  0.0 49.7 jit_solution(18124603809953652942)
XLA Ops:
  0.6 44.1 %shard_map.85 = (bf16[16,8,8,512]{3,2,1,0:T(8,128)(2,1)}, bf16[16,8,8,512]{3,2,1,0:T(8,128)(2,1)}, bf16[16,8,8,512]{3,2,1,0:T(8,128)(2,1)}) custom-call(bf16[16,8,8,512]{3,2,1,0:T(8,128)(2,1)} %bitcast.12, bf16[16,8,8,512]{3,2,1,0:T(8,128)(2,1)} %bitcast.13, bf16[16,8,8,512]{3,2,1,0:T(8,128)(2,1)} %bitcast.14, bf16[16,8,8,512]{3,2,1,0:T(8,128)(2,1)} %bitcast.15, ...), custom_call_target="tpu_custom_call" | custom-call | tf_op jit(solution)/shard_map/pallas_call | solution.py:473
  44.7 0.0 copy-start.1
  44.7 2.4 %copy.12 = bf16[16,64,512]{2,1,0:T(8,128)(2,1)} copy(bf16[16,64,512]{2,1,0:T(8,128)(2,1)} %bitcast.11) | data formatting | bytes 2097152
  47.1 0.0 copy-done.1
  47.1 0.0 copy-start
  47.1 1.0 %copy.13 = bf16[16,64,512]{2,1,0:T(8,128)(2,1)} copy(bf16[16,64,512]{2,1,0:T(8,128)(2,1)S(1)} %bitcast.10) | data formatting | bytes 2097152
  48.1 0.6 %copy-done = bf16[16,8,8,512]{3,2,1,0:T(8,128)(2,1)S(1)} copy-done((bf16[16,8,8,512]{3,2,1,0:T(8,128)(2,1)S(1)}, bf16[16,8,8,512]{3,2,1,0:T(8,128)(2,1)}, u32[]{:S(2)}) %copy-start) | copy-done | bytes 1048600
  48.7 1.0 %copy.14 = bf16[16,64,512]{2,1,0:T(8,128)(2,1)} copy(bf16[16,64,512]{2,1,0:T(8,128)(2,1)S(1)} %bitcast.9) | data formatting | bytes 2097152
Async XLA Ops:
  44.7 2.4 %copy-start.1 = (bf16[16,8,8,512]{3,2,1,0:T(8,128)(2,1)S(1)}, bf16[16,8,8,512]{3,2,1,0:T(8,128)(2,1)}, u32[]{:S(2)}) copy-start(bf16[16,8,8,512]{3,2,1,0:T(8,128)(2,1)} %get-tuple-element.7) | copy-start | bytes 3145732
  47.1 1.6 %copy-start = (bf16[16,8,8,512]{3,2,1,0:T(8,128)(2,1)S(1)}, bf16[16,8,8,512]{3,2,1,0:T(8,128)(2,1)}, u32[]{:S(2)}) copy-start(bf16[16,8,8,512]{3,2,1,0:T(8,128)(2,1)} %get-tuple-element.8) | copy-start | bytes 3145732

commit v2 on v1

--- a/solution.py
+++ b/solution.py
@@ -13,6 +13,9 @@
 BIG = 32768.0
 EXP_SCALE = 0.125 * 1.4426950408889634
 CHUNKS = 2
+LAG1 = 2
+LAG2 = 2
+PER = 2
 
 
 def _iota(shape, dim):
@@ -31,8 +34,8 @@
     return x.reshape(-1, x.shape[-1])
 
 
-def _key_features(base, row0, rows, q_base, total):
-    shape = (2 * rows * 8, 128)
+def _key_features(base, row0, rows, q_base, total, tiles, spread):
+    shape = (tiles * rows * 8, 128)
     key = _iota(shape, 0)
     lane = _iota(shape, 1)
     tile = key // (rows * 8)
@@ -42,10 +45,12 @@
     q_row = q_base + 2 * group + slot - 6
     first = jnp.clip(q_row - 3, 0, total - 7)
     row_ok = (k_row >= first) & (k_row < first + 7)
-    gap = k_col - 4 - group
+    gap = k_col - 4 - group - jnp.where(slot == 9, spread, 0)
     col_ok = (gap >= -3) & (gap <= 3)
     row_slot = (slot == 6) | (slot == 7)
-    bad = (row_slot & jnp.logical_not(row_ok)) | ((slot == 8) & jnp.logical_not(col_ok))
+    bad = (row_slot & jnp.logical_not(row_ok)) | (
+        ((slot == 8) | (slot == 9)) & jnp.logical_not(col_ok)
+    )
     value = jnp.where(bad, -BIG, jnp.where(slot < 3, -8.0, 0.0))
     return value.astype(BF)
 
@@ -202,9 +207,9 @@
     low = _iota((1, 128), 1) < 64
     head_keep = [(group16 == h) | (slot16 >= 6) for h in range(8)]
     for t in range(2):
-        feat[t] = _key_features(base, 8 * t, 8, base, total)
-    feat_halo[0] = _key_features(base, 0, 4, base - 16, total)
-    feat_halo[1] = _key_features(base, 12, 4, base + 16, total)
+        feat[t] = _key_features(base, 8 * t, 8, base, total, 2, 0)
+    feat_halo[0] = _key_features(base, 0, 4, base - 16, total, 3, 8)
+    feat_halo[1] = _key_features(base, 12, 4, base + 16, total, 3, 8)
 
     @pl.loop(0, 9)
     def _(tile):
@@ -227,7 +232,8 @@
     column = _iota((64, 128), 0) % 8
     group = _iota((64, 128), 1) // 16
     slot = _iota((64, 128), 1) % 16
-    col_hot = jnp.where((slot == 8) & (group == column), 1.0, 0.0)
+    odd = _iota((64, 128), 0) // 8 % 2
+    col_hot = jnp.where((slot == 8 + odd) & (group == column), 1.0, 0.0)
 
     def features_of(r):
         product = _flat(gv[r].astype(F32)) * _flat(ov[r].astype(F32))
@@ -269,7 +275,7 @@
     def two(x):
         return jnp.concatenate([_keep(low, x), _keep(jnp.logical_not(low), x)], axis=0)
 
-    def unit(s, t, p):
+    def front(s, t, p):
         lanes = pl.ds(128 * p, 128)
         k_rows = pl.ds(8 * t, 8)
         q_rows = pl.ds(4 * t, 12)
@@ -295,33 +301,58 @@
             jnp.concatenate([g2, a2], axis=1),
             ((1,), (1,)),
         )
+        return scores, prob_grad, q2, g2, keys
+
+    def middle(scores, prob_grad, q2, g2, keys):
         weights = jnp.exp2(scores * EXP_SCALE)
         score_grad = (weights * prob_grad).astype(BF)
+        turned_grad = score_grad.T
+        turned_grad = jnp.concatenate([turned_grad[:96], turned_grad[96:]], axis=1)
+        return weights.astype(BF), score_grad, turned_grad, q2, g2, keys
+
+    def back(s, t, p, weights, score_grad, turned_grad, q2, g2, keys):
+        lanes = pl.ds(128 * p, 128)
+        k_rows = pl.ds(8 * t, 8)
         d_keys = _dot(score_grad, q2, ((1,), (0,)))
-        d_values = _dot(weights.astype(BF), g2, ((1,), (0,)))
-        turned_grad = score_grad.T
-        d_query = _dot(
-            jnp.concatenate([turned_grad[:96], turned_grad[96:]], axis=1),
-            two(keys),
-            ((1,), (0,)),
-        )
+        d_values = _dot(weights, g2, ((1,), (0,)))
+        d_query = _dot(turned_grad, two(keys), ((1,), (0,)))
         for acc, d in ((dk_acc, d_keys), (dv_acc, d_values)):
             acc[s, k_rows, :, lanes] += d[:64].reshape(8, 8, 128)
             acc[s + 1, k_rows, :, lanes] += d[64:].reshape(8, 8, 128)
         return d_query
 
-    def strip(s):
-        for p in range(4):
+    def pipelined(todo, one, two_, three, use):
+        n = len(todo)
+        first, second = {}, {}
+        for i in range(n + LAG1 + LAG2):
+            if i < n:
+                first[i] = one(*todo[i])
+            j = i - LAG1
+            if 0 <= j < n:
+                second[j] = two_(*first.pop(j))
+            j = i - LAG1 - LAG2
+            if 0 <= j < n:
+                use(j, three(*todo[j], *second.pop(j)))
+
+    def strips(which):
+        todo = [(s, t, p) for s in which for p in range(4) for t in range(2)]
+        upper = [None]
+
+        def use(j, d_query):
+            s, t, p = todo[j]
+            if t == 0:
+                upper[0] = d_query
+                return
             lanes = pl.ds(128 * p, 128)
-            upper = unit(s, 0, p)
-            lower = unit(s, 1, p)
-            dq_acc[pl.ds(0, 4), s, :, lanes] = upper[:32].reshape(4, 8, 128)
-            dq_acc[pl.ds(4, 8), s, :, lanes] = (upper[32:] + lower[:64]).reshape(8, 8, 128)
-            dq_acc[pl.ds(12, 4), s, :, lanes] = lower[64:].reshape(4, 8, 128)
-
-    @pl.loop(1, 7)
-    def _(s):
-        strip(s)
+            dq_acc[pl.ds(0, 4), s, :, lanes] = upper[0][:32].reshape(4, 8, 128)
+            dq_acc[pl.ds(4, 8), s, :, lanes] = (upper[0][32:] + d_query[:64]).reshape(8, 8, 128)
+            dq_acc[pl.ds(12, 4), s, :, lanes] = d_query[64:].reshape(4, 8, 128)
+
+        pipelined(todo, front, middle, back, use)
+
+    @pl.loop(0, 6 // PER)
+    def _(i):
+        strips([1 + PER * i + j for j in range(PER)])
 
     for what in range(2):
         for side in range(2):
@@ -330,55 +361,63 @@
         dst[0] = jnp.where(half, turned(rim_in[0, i]), turned(src[:, 0])).astype(BF)
         dst[8] = jnp.where(half, turned(src[:, 7]), turned(rim_in[1, i])).astype(BF)
 
-    @pl.loop(0, 2)
-    def _(i):
-        strip(7 * i)
-
-    lane512 = _iota((1, 512), 1)
-    prob_halo = _prob_features(64)
-
-    def halo_unit(s, side):
+    strips([0, 7])
+
+    prob_halo = _prob_features(96)
+
+    def keys_of(ref, s, rows, lanes):
+        return jnp.concatenate([_flat(ref[s + i, rows, :, lanes]) for i in range(3)], axis=0)
+
+    def queries_of(ref, side, s, lanes):
+        return jnp.concatenate([_flat(ref[side, :, s + i, :, lanes]) for i in range(2)], axis=0)
+
+    def halo_front(s, side, p):
+        lanes = pl.ds(128 * p, 128)
         rows = pl.ds(12 * side, 4)
-        keys = jnp.concatenate([_flat(ksh[s, rows]), _flat(ksh[s + 1, rows])], axis=0)
-        values = jnp.concatenate([_flat(vsh[s, rows]), _flat(vsh[s + 1, rows])], axis=0)
-        q = _flat(q_halo[side, :, s])
-        g = _flat(g_halo[side, :, s])
-        extra = _flat(a_halo[side, :, s])
-        q8 = jnp.concatenate([_keep(lane512 // 64 == h, q) for h in range(8)], axis=0)
-        g8 = jnp.concatenate([_keep(lane512 // 64 == h, g) for h in range(8)], axis=0)
-        a8 = jnp.concatenate([_keep(head_keep[h], extra) for h in range(8)], axis=0)
+        keys = keys_of(ksh, s, rows, lanes)
+        values = keys_of(vsh, s, rows, lanes)
+        q2 = two(queries_of(q_halo, side, s, lanes))
+        g2 = two(queries_of(g_halo, side, s, lanes))
+        extra = queries_of(a_halo, side, s, pl.ds(0, 128))
+        a2 = jnp.concatenate(
+            [_keep(head_keep[2 * p], extra), _keep(head_keep[2 * p + 1], extra)], axis=0
+        )
         scores = _dot(
             jnp.concatenate([keys, feat_halo[side]], axis=1),
-            jnp.concatenate([q8, a8], axis=1),
+            jnp.concatenate([q2, a2], axis=1),
             ((1,), (1,)),
         )
         prob_grad = _dot(
             jnp.concatenate([values, prob_halo], axis=1),
-            jnp.concatenate([g8, a8], axis=1),
+            jnp.concatenate([g2, a2], axis=1),
             ((1,), (1,)),
         )
+        return scores, prob_grad, q2, g2, keys
+
+    def halo_middle(scores, prob_grad, q2, g2, keys):
         weights = jnp.exp2(scores * EXP_SCALE)
         score_grad = (weights * prob_grad).astype(BF)
-        d_keys = _dot(score_grad, q8, ((1,), (0,)))
-        d_values = _dot(weights.astype(BF), g8, ((1,), (0,)))
-        turned_grad = score_grad.T
-        for p in range(4):
-            lanes = slice(128 * p, 128 * p + 128)
-            d_query = _dot(turned_grad[64 * p : 64 * p + 64], keys[:, lanes], ((1,), (0,)))
-            d_query = jnp.where(low, d_query[:32], d_query[32:]) * 0.125
-            dq_send[side, :, s, :, lanes] = d_query[:24].reshape(3, 8, 128).astype(BF)
+        return weights.astype(BF), score_grad, score_grad.T, q2, g2, keys
+
+    def halo_back(s, side, p, weights, score_grad, turned_grad, q2, g2, keys):
+        lanes = pl.ds(128 * p, 128)
+        rows = pl.ds(12 * side, 4)
+        d_keys = _dot(score_grad, q2, ((1,), (0,)))
+        d_values = _dot(weights, g2, ((1,), (0,)))
+        d_query = _dot(turned_grad, keys, ((1,), (0,)))
+        d_query = jnp.where(low, d_query[:64], d_query[64:]) * 0.125
+        for i in range(2):
+            part = d_query[32 * i : 32 * i + 24].reshape(3, 8, 128)
+            dq_send[side, :, s + i, :, lanes] = part.astype(BF)
         for acc, d in ((dk_acc, d_keys), (dv_acc, d_values)):
-            acc[s, rows] += d[:32].reshape(4, 8, 512)
-            acc[s + 1, rows] += d[32:].reshape(4, 8, 512)
+            for i in range(3):
+                acc[s + i, rows, :, lanes] += d[32 * i : 32 * i + 32].reshape(4, 8, 128)
 
     def halo(chunk, side):
         for what in range(3):
             row_copy(what, chunk, side).wait_recv()
-
-        @pl.loop(chunk * width, (chunk + 1) * width)
-        def _(s):
-            halo_unit(s, side)
-
+        todo = [(s, side, p) for s in range(chunk * width, (chunk + 1) * width, 2) for p in range(4)]
+        pipelined(todo, halo_front, halo_middle, halo_back, lambda j, done: None)
         back_copy(chunk, side).start()
 
     for chunk in range(CHUNKS):
@@ -489,7 +528,7 @@
                 pltpu.VMEM(shifted, F32),
                 pltpu.VMEM(shifted, F32),
                 pltpu.VMEM((2, 128, 128), BF),
-                pltpu.VMEM((2, 64, 128), BF),
+                pltpu.VMEM((2, 96, 128), BF),
                 pltpu.VMEM((2, 2, 16, 8, 512), BF),
                 pltpu.VMEM((2, 4, 8, 8, 512), BF),
                 pltpu.VMEM((2, 4, 8, 8, 512), BF),

time: 49.8 us -> 40.8 us (0.82)
  the two profiles are of different devices: /device:TPU:17 before, /device:TPU:1 now
where the time goes in v2:
time: 40.8 us; the launch traced here: 40.7 us
  Pallas kernels  35.1 us (86%)
  local copies, waits for them, and re-layouts  4.95 us (12%)
  between operations  0.65 us (2%)
    pallas_call x1, Pallas kernels, per_device(): pl.pallas_call(functools.partial(kernel, n_lat, n_lon), out_shape=[jax.Sh...  35.1 us
    unnamed x7, local copies, waits for them, and re-layouts  4.95 us

profile of v2, /device:TPU:1, one launch (start us, length us, event | category | flops | bytes accessed | tf_op | source)
XLA Modules:
  0.0 40.7 jit_solution(17361209594001781432)
XLA Ops:
  0.6 35.1 %shard_map.85 = (bf16[16,8,8,512]{3,2,1,0:T(8,128)(2,1)}, bf16[16,8,8,512]{3,2,1,0:T(8,128)(2,1)}, bf16[16,8,8,512]{3,2,1,0:T(8,128)(2,1)}) custom-call(bf16[16,8,8,512]{3,2,1,0:T(8,128)(2,1)} %bitcast.12, bf16[16,8,8,512]{3,2,1,0:T(8,128)(2,1)} %bitcast.13, bf16[16,8,8,512]{3,2,1,0:T(8,128)(2,1)} %bitcast.14, bf16[16,8,8,512]{3,2,1,0:T(8,128)(2,1)} %bitcast.15, ...), custom_call_target="tpu_custom_call" | custom-call | tf_op jit(solution)/shard_map/pallas_call | solution.py:512
  35.7 0.0 copy-start.1
  35.7 2.4 %copy.12 = bf16[16,64,512]{2,1,0:T(8,128)(2,1)} copy(bf16[16,64,512]{2,1,0:T(8,128)(2,1)} %bitcast.11) | data formatting | bytes 2097152
  38.1 0.0 copy-done.1
  38.1 0.0 copy-start
  38.1 1.0 %copy.13 = bf16[16,64,512]{2,1,0:T(8,128)(2,1)} copy(bf16[16,64,512]{2,1,0:T(8,128)(2,1)S(1)} %bitcast.10) | data formatting | bytes 2097152
  39.1 0.6 %copy-done = bf16[16,8,8,512]{3,2,1,0:T(8,128)(2,1)S(1)} copy-done((bf16[16,8,8,512]{3,2,1,0:T(8,128)(2,1)S(1)}, bf16[16,8,8,512]{3,2,1,0:T(8,128)(2,1)}, u32[]{:S(2)}) %copy-start) | copy-done | bytes 1048600
  39.7 1.0 %copy.14 = bf16[16,64,512]{2,1,0:T(8,128)(2,1)} copy(bf16[16,64,512]{2,1,0:T(8,128)(2,1)S(1)} %bitcast.9) | data formatting | bytes 2097152
Async XLA Ops:
  35.7 2.4 %copy-start.1 = (bf16[16,8,8,512]{3,2,1,0:T(8,128)(2,1)S(1)}, bf16[16,8,8,512]{3,2,1,0:T(8,128)(2,1)}, u32[]{:S(2)}) copy-start(bf16[16,8,8,512]{3,2,1,0:T(8,128)(2,1)} %get-tuple-element.7) | copy-start | bytes 3145732
  38.1 1.6 %copy-start = (bf16[16,8,8,512]{3,2,1,0:T(8,128)(2,1)S(1)}, bf16[16,8,8,512]{3,2,1,0:T(8,128)(2,1)}, u32[]{:S(2)}) copy-start(bf16[16,8,8,512]{3,2,1,0:T(8,128)(2,1)} %get-tuple-element.8) | copy-start | bytes 3145732

commit v3 on v2

--- a/solution.py
+++ b/solution.py
@@ -16,6 +16,7 @@
 LAG1 = 2
 LAG2 = 2
 PER = 2
+RELAY_STEPS = (((0, 0), (1, 0)), ((0, 1), (2, 0)), ((1, 1), (2, 1)))
 
 
 def _iota(shape, dim):
@@ -115,6 +116,15 @@
     below = (lat + 1, lon)
     has_above = lat > 0
     has_below = lat < n_lat - 1
+    middle_band = n_lat // 2
+    relayed = n_lat >= 4 and n_lat % 2 == 0 and n_lon % 4 == 0
+    across = lon + 2 - 4 * (lon // 2 % 2) if relayed else lon
+    near_middle = [lat == middle_band - 1, lat == middle_band] if relayed else [False, False]
+    is_relay = [lat == 0, lat == n_lat - 1] if relayed else [False, False]
+
+    def as_int(condition):
+        return jnp.where(condition, 1, 0)
+
     total = n_lat * 16
     base = lat * 16
     width = 8 // CHUNKS
@@ -137,36 +147,84 @@
     greet(right)
     pl.when(has_above)(lambda: greet(above))
     pl.when(has_below)(lambda: greet(below))
-    peers = 2 + jnp.minimum(lat, 1) + jnp.minimum(n_lat - 1 - lat, 1)
+    peers = 2 + as_int(has_above) + as_int(has_below)
+    if relayed:
+        for place, partners in (
+            (near_middle[0] | near_middle[1], (0, n_lat - 1)),
+            (is_relay[0] | is_relay[1], (middle_band - 1, middle_band)),
+        ):
+            peers += 2 * as_int(place)
+            for partner in partners:
+                pl.when(place)(functools.partial(greet, (partner, across)))
     pl.semaphore_wait(barrier, peers)
 
-    def remote(src, dst, sems, index, device):
+    def remote(src, dst, sems, index, device, landing=None):
         return pltpu.make_async_remote_copy(
             src_ref=src,
             dst_ref=dst,
             send_sem=sems.at[(0,) + index],
-            recv_sem=sems.at[(1,) + index],
+            recv_sem=sems.at[(1,) + (index if landing is None else landing)],
             device_id=device,
             device_id_type=MESH,
         )
 
+    row_buffers = ((q_hbm, q_halo), (g_hbm, g_halo), (aug, a_halo))
+
     def row_copy(what, chunk, side):
-        src, dst = ((q_hbm, q_halo), (g_hbm, g_halo), (aug, a_halo))[what]
+        src, dst = row_buffers[what]
         rows = pl.ds(13, 3) if side == 0 else pl.ds(0, 3)
         strips = pl.ds(chunk * width, width)
+        device, slot = (below, above)[side], side
+        if relayed:
+            turn = as_int(near_middle[side])
+            hop = middle_band - 1 if side == 1 else n_lat - 1 - middle_band
+            direction = 1 - 2 * side
+            device = (
+                lat + direction * (1 + turn * hop),
+                lon + turn * (across - lon),
+            )
+            slot = side + direction * turn
         return remote(
             src.at[rows, strips],
-            dst.at[side, pl.ds(0, 3), strips],
+            dst.at[slot, pl.ds(0, 3), strips],
             row_sems,
             (what, chunk, side),
-            below if side == 0 else above,
-        )
+            device,
+            (what, chunk, slot),
+        )
+
+    def row_forward(what, chunk, side):
+        buffer = row_buffers[what][1]
+        strips = pl.ds(chunk * width, width)
+        return remote(
+            buffer.at[side, pl.ds(0, 3), strips],
+            buffer.at[1 - side, pl.ds(0, 3), strips],
+            row_sems,
+            (what, chunk, 1 - side),
+            (middle_band - 1 + side, across),
+        )
+
+    def await_rows(what, chunk, side):
+        buffer = row_buffers[what][1]
+        rows = buffer.at[side, pl.ds(0, 3), pl.ds(chunk * width, width)]
+        remote(rows, rows, row_sems, (what, chunk, side), left).wait_recv()
+
+    def forward(pieces):
+        if not relayed:
+            return
+        for side in range(2):
+
+            @pl.when(is_relay[side])
+            def _():
+                for what, chunk in pieces:
+                    await_rows(what, chunk, side)
+                    row_forward(what, chunk, side).start()
 
     def rim_copy(what, side):
         src = (k_hbm, v_hbm)[what]
         return remote(
-            src.at[:, 7 if side == 0 else 0],
-            rim_in.at[side, what],
+            src.at[:, 7 if side == 0 else 0, pl.ds(4 if side == 0 else 0, 4)],
+            rim_in.at[side, what, :, pl.ds(4 if side == 0 else 0, 4)],
             rim_sems,
             (what, side),
             right if side == 0 else left,
@@ -353,6 +411,8 @@
     @pl.loop(0, 6 // PER)
     def _(i):
         strips([1 + PER * i + j for j in range(PER)])
+        for step, pieces in enumerate(RELAY_STEPS):
+            pl.when(i == step)(functools.partial(forward, pieces))
 
     for what in range(2):
         for side in range(2):
@@ -415,7 +475,7 @@
 
     def halo(chunk, side):
         for what in range(3):
-            row_copy(what, chunk, side).wait_recv()
+            await_rows(what, chunk, side)
         todo = [(s, side, p) for s in range(chunk * width, (chunk + 1) * width, 2) for p in range(4)]
         pipelined(todo, halo_front, halo_middle, halo_back, lambda j, done: None)
         back_copy(chunk, side).start()
@@ -495,8 +555,28 @@
                 row_copy(what, chunk, send_side).wait_send()
             back_copy(chunk, back_side).wait_send()
 
+    if relayed:
+        for side in range(2):
+
+            @pl.when(is_relay[side])
+            def _():
+                for pieces in RELAY_STEPS:
+                    for what, chunk in pieces:
+                        row_forward(what, chunk, side).wait_send()
+
     pl.when(has_below)(lambda: drain(0, 1))
     pl.when(has_above)(lambda: drain(1, 0))
+
+
+def store_kernel(a, b, c, a_out, b_out, c_out, sem):
+    copies = [
+        pltpu.make_async_copy(src, dst, sem.at[i])
+        for i, (src, dst) in enumerate(((a, a_out), (b, b_out), (c, c_out)))
+    ]
+    for copy in copies:
+        copy.start()
+    for copy in copies:
+        copy.wait()
 
 
 def solution(mesh):
@@ -511,8 +591,8 @@
         shifted = (9, 16, 8, 512)
         outs = pl.pallas_call(
             functools.partial(kernel, n_lat, n_lon),
-            out_shape=[jax.ShapeDtypeStruct(token, BF)] * 3,
-            in_specs=[pl.BlockSpec(memory_space=pl.ANY)] * 6,
+            out_shape=[pltpu.VMEM(token, BF)] * 3,
+            in_specs=[pl.BlockSpec(memory_space=pltpu.HBM)] * 6,
             out_specs=[pl.BlockSpec(memory_space=pltpu.VMEM)] * 3,
             scratch_shapes=[
                 pltpu.VMEM(token, BF),
@@ -556,6 +636,14 @@
             tiled(grad_output),
             log_totals.reshape(128, 64),
         )
+        outs = pl.pallas_call(
+            store_kernel,
+            out_shape=[jax.ShapeDtypeStruct(token, BF)] * 3,
+            in_specs=[pl.BlockSpec(memory_space=pltpu.VMEM)] * 3,
+            out_specs=[pl.BlockSpec(memory_space=pltpu.HBM)] * 3,
+            scratch_shapes=[dma((3,))],
+            compiler_params=pltpu.CompilerParams(vmem_limit_bytes=8 * 1024 * 1024),
+        )(*outs)
         return tuple(x.reshape(16, 64, 512) for x in outs)
 
     return jax.shard_map(

time: 40.8 us -> 37 us (0.907)
  local copies, waits for them, and re-layouts: 4.95 us -> 0 us
  Pallas kernels: 35.1 us -> 36.3 us
    unnamed x7 -> x0, local copies, waits for them, and re-layouts: 4.95 us -> none
    pallas_call x1 -> x2, Pallas kernels: 35.1 us -> 36.3 us  [the longest x1 34.6 us: per_device(): pl.pallas_call(functools.partial(kernel, n_lat, n_lon), out_shape=[pltpu....]
where the time goes in v3:
time: 37 us
  Pallas kernels  36.3 us (98%)
  between operations  0.64 us (2%)
    pallas_call x1, Pallas kernels, per_device(): pl.pallas_call(functools.partial(kernel, n_lat, n_lon), out_shape=[pltpu....  34.6 us
    pallas_call x1, Pallas kernels, per_device(): pl.pallas_call(store_kernel, out_shape=[jax.ShapeDtypeStruct(token, BF)]...  1.69 us

profile of v3, /device:TPU:1, one launch (start us, length us, event | category | flops | bytes accessed | tf_op | source)
XLA Modules:
  0.0 37.0 jit_solution(4980383602339588252)
XLA Ops:
  0.6 34.6 %shard_map.85 = (bf16[16,8,8,512]{3,2,1,0:T(8,128)(2,1)S(1)}, bf16[16,8,8,512]{3,2,1,0:T(8,128)(2,1)S(1)}, bf16[16,8,8,512]{3,2,1,0:T(8,128)(2,1)S(1)}) custom-call(bf16[16,8,8,512]{3,2,1,0:T(8,128)(2,1)} %bitcast.9, bf16[16,8,8,512]{3,2,1,0:T(8,128)(2,1)} %bitcast.10, bf16[16,8,8,512]{3,2,1,0:T(8,128)(2,1)} %bitcast.11, bf16[16,8,8,512]{3,2,1,0:T(8,128)(2,1)} %bitcast.12, ...), custom_call_target="tpu_custom_call" | custom-call | tf_op jit(solution)/shard_map/pallas_call | solution.py:592
  35.3 1.7 %shard_map.86 = (bf16[16,8,8,512]{3,2,1,0:T(8,128)(2,1)}, bf16[16,8,8,512]{3,2,1,0:T(8,128)(2,1)}, bf16[16,8,8,512]{3,2,1,0:T(8,128)(2,1)}) custom-call(bf16[16,8,8,512]{3,2,1,0:T(8,128)(2,1)S(1)} %get-tuple-element.9.a, bf16[16,8,8,512]{3,2,1,0:T(8,128)(2,1)S(1)} %get-tuple-element.10.b, bf16[16,8,8,512]{3,2,1,0:T(8,128)(2,1)S(1)} %get-tuple-element.11.c), custom_call_target="tpu_custom_call" | custom-call | tf_op jit(solution)/shard_map/pallas_call | solution.py:639

commit v4 on v3

--- a/solution.py
+++ b/solution.py
@@ -15,7 +15,6 @@
 CHUNKS = 2
 LAG1 = 2
 LAG2 = 2
-PER = 2
 RELAY_STEPS = (((0, 0), (1, 0)), ((0, 1), (2, 0)), ((1, 1), (2, 1)))
 
 
@@ -107,6 +106,7 @@
     row_sems,
     back_sems,
     grad_sems,
+    ready,
 ):
     lat = lax.axis_index("lat")
     lon = lax.axis_index("lon")
@@ -145,18 +145,26 @@
 
     greet(left)
     greet(right)
+    greets_below = has_below & jnp.logical_not(near_middle[0]) if relayed else has_below
     pl.when(has_above)(lambda: greet(above))
-    pl.when(has_below)(lambda: greet(below))
+    pl.when(greets_below)(lambda: greet(below))
     peers = 2 + as_int(has_above) + as_int(has_below)
     if relayed:
         for place, partners in (
-            (near_middle[0] | near_middle[1], (0, n_lat - 1)),
-            (is_relay[0] | is_relay[1], (middle_band - 1, middle_band)),
+            (is_relay[0], (middle_band - 1, middle_band)),
+            (is_relay[1], (middle_band - 1,)),
+            (near_middle[1], (n_lat - 1,)),
         ):
-            peers += 2 * as_int(place)
             for partner in partners:
                 pl.when(place)(functools.partial(greet, (partner, across)))
+        peers += 2 * as_int(near_middle[0]) + as_int(is_relay[1])
     pl.semaphore_wait(barrier, peers)
+    if relayed:
+
+        @pl.when(near_middle[0])
+        def _():
+            for device in ((0, across), below):
+                pl.semaphore_signal(ready, inc=1, device_id=device, device_id_type=MESH)
 
     def remote(src, dst, sems, index, device, landing=None):
         return pltpu.make_async_remote_copy(
@@ -209,13 +217,15 @@
         rows = buffer.at[side, pl.ds(0, 3), pl.ds(chunk * width, width)]
         remote(rows, rows, row_sems, (what, chunk, side), left).wait_recv()
 
-    def forward(pieces):
+    def forward(pieces, first=False):
         if not relayed:
             return
         for side in range(2):
 
             @pl.when(is_relay[side])
             def _():
+                if first and side == 0:
+                    pl.semaphore_wait(ready, 1)
                 for what, chunk in pieces:
                     await_rows(what, chunk, side)
                     row_forward(what, chunk, side).start()
@@ -237,7 +247,7 @@
             dq_recv.at[1 - side, :, strips],
             back_sems,
             (chunk, 1 - side),
-            above if side == 0 else below,
+            (lat - 1 + 2 * side, lon),
         )
 
     def grad_copy(what, side):
@@ -249,13 +259,23 @@
             right if side == 0 else left,
         )
 
-    def send_rows(whats, side):
-        for chunk in range(CHUNKS):
+    has = (has_above, has_below)
+
+    def send_rows(whats, side, chunks):
+        for chunk in chunks:
             for what in whats:
                 row_copy(what, chunk, side).start()
 
-    pl.when(has_below)(lambda: send_rows((0, 1), 0))
-    pl.when(has_above)(lambda: send_rows((0, 1), 1))
+    every = range(CHUNKS)
+    for side in range(2):
+        if relayed:
+            pl.when(near_middle[side])(functools.partial(send_rows, (0, 1), side, every))
+    for chunk in every:
+        for side in range(2):
+            first = has[1 - side]
+            if relayed:
+                first = first & jnp.logical_not(near_middle[side])
+            pl.when(first)(functools.partial(send_rows, (0, 1), side, (chunk,)))
     for what in range(2):
         for side in range(2):
             rim_copy(what, side).start()
@@ -307,10 +327,10 @@
 
     for r in (13, 14, 15):
         features_of(r)
-    pl.when(has_below)(lambda: send_rows((2,), 0))
+    pl.when(has_below)(lambda: send_rows((2,), 0, every))
     for r in (0, 1, 2):
         features_of(r)
-    pl.when(has_above)(lambda: send_rows((2,), 1))
+    pl.when(has_above)(lambda: send_rows((2,), 1, every))
     for r in range(3, 13):
         features_of(r)
 
@@ -408,11 +428,10 @@
 
         pipelined(todo, front, middle, back, use)
 
-    @pl.loop(0, 6 // PER)
-    def _(i):
-        strips([1 + PER * i + j for j in range(PER)])
-        for step, pieces in enumerate(RELAY_STEPS):
-            pl.when(i == step)(functools.partial(forward, pieces))
+    strips([1, 2])
+    forward(RELAY_STEPS[0], True)
+    strips([3, 4])
+    forward(RELAY_STEPS[1])
 
     for what in range(2):
         for side in range(2):
@@ -422,6 +441,7 @@
         dst[8] = jnp.where(half, turned(src[:, 7]), turned(rim_in[1, i])).astype(BF)
 
     strips([0, 7])
+    forward(RELAY_STEPS[2])
 
     prob_halo = _prob_features(96)
 
@@ -473,16 +493,29 @@
             for i in range(3):
                 acc[s + i, rows, :, lanes] += d[32 * i : 32 * i + 32].reshape(4, 8, 128)
 
-    def halo(chunk, side):
-        for what in range(3):
-            await_rows(what, chunk, side)
-        todo = [(s, side, p) for s in range(chunk * width, (chunk + 1) * width, 2) for p in range(4)]
-        pipelined(todo, halo_front, halo_middle, halo_back, lambda j, done: None)
-        back_copy(chunk, side).start()
-
-    for chunk in range(CHUNKS):
-        pl.when(has_above)(functools.partial(halo, chunk, 0))
-        pl.when(has_below)(functools.partial(halo, chunk, 1))
+    @pl.loop(0, 2 * CHUNKS)
+    def _(k):
+        chunk, side = k // 2, k % 2
+        if relayed:
+            middle_one = as_int(near_middle[0] | near_middle[1])
+            chunk = chunk + middle_one * (k % CHUNKS - chunk)
+            side = side + middle_one * (k // CHUNKS - side)
+            turn = as_int(near_middle[1])
+            side = side + turn * (1 - 2 * side)
+
+        @pl.when(has_above & (side == 0) | has_below & (side == 1))
+        def _():
+            for what in range(3):
+                await_rows(what, chunk, side)
+            todo = [(chunk * width + 2 * i, side, p) for i in range(width // 2) for p in range(4)]
+            pipelined(todo, halo_front, halo_middle, halo_back, lambda j, done: None)
+            if relayed:
+
+                @pl.when(near_middle[1] & (side == 0) & (chunk == 0))
+                def _():
+                    pl.semaphore_wait(ready, 1)
+
+            back_copy(chunk, side).start()
 
     half8 = _iota((1, 8, 512), 1) < 4
     for what, acc in enumerate((dk_acc, dv_acc)):
@@ -498,6 +531,8 @@
             ).astype(BF)
         for side in range(2):
             grad_copy(what, side).start()
+
+    strips([5, 6])
 
     @pl.loop(3, 13)
     def _(r):
@@ -622,6 +657,7 @@
                 dma((2, 3, CHUNKS, 2)),
                 dma((2, CHUNKS, 2)),
                 dma((2, 2, 2)),
+                pltpu.SemaphoreType.REGULAR,
             ],
             compiler_params=pltpu.CompilerParams(
                 collective_id=0,

time: 37 us -> 33.8 us (0.914)
  the two profiles are of different devices: /device:TPU:1 before, /device:TPU:25 now
where the time goes in v4:
time: 33.8 us; the launch traced here: 33.7 us
  Pallas kernels  33.1 us (98%)
  between operations  0.64 us (2%)
    pallas_call x1, Pallas kernels, per_device(): pl.pallas_call(functools.partial(kernel, n_lat, n_lon), out_shape=[pltpu....  31.4 us
    pallas_call x1, Pallas kernels, per_device(): pl.pallas_call(store_kernel, out_shape=[jax.ShapeDtypeStruct(token, BF)]...  1.69 us

profile of v4, /device:TPU:25, one launch (start us, length us, event | category | flops | bytes accessed | tf_op | source)
XLA Modules:
  0.0 33.7 jit_solution(9640530013033108604)
XLA Ops:
  0.6 31.4 %shard_map.85 = (bf16[16,8,8,512]{3,2,1,0:T(8,128)(2,1)S(1)}, bf16[16,8,8,512]{3,2,1,0:T(8,128)(2,1)S(1)}, bf16[16,8,8,512]{3,2,1,0:T(8,128)(2,1)S(1)}) custom-call(bf16[16,8,8,512]{3,2,1,0:T(8,128)(2,1)} %bitcast.9, bf16[16,8,8,512]{3,2,1,0:T(8,128)(2,1)} %bitcast.10, bf16[16,8,8,512]{3,2,1,0:T(8,128)(2,1)} %bitcast.11, bf16[16,8,8,512]{3,2,1,0:T(8,128)(2,1)} %bitcast.12, ...), custom_call_target="tpu_custom_call" | custom-call | tf_op jit(solution)/shard_map/pallas_call | solution.py:627
  32.0 1.7 %shard_map.86 = (bf16[16,8,8,512]{3,2,1,0:T(8,128)(2,1)}, bf16[16,8,8,512]{3,2,1,0:T(8,128)(2,1)}, bf16[16,8,8,512]{3,2,1,0:T(8,128)(2,1)}) custom-call(bf16[16,8,8,512]{3,2,1,0:T(8,128)(2,1)S(1)} %get-tuple-element.9.a, bf16[16,8,8,512]{3,2,1,0:T(8,128)(2,1)S(1)} %get-tuple-element.10.b, bf16[16,8,8,512]{3,2,1,0:T(8,128)(2,1)S(1)} %get-tuple-element.11.c), custom_call_target="tpu_custom_call" | custom-call | tf_op jit(solution)/shard_map/pallas_call | solution.py:675

commit v5 on v4

--- a/solution.py
+++ b/solution.py
@@ -15,7 +15,6 @@
 CHUNKS = 2
 LAG1 = 2
 LAG2 = 2
-RELAY_STEPS = (((0, 0), (1, 0)), ((0, 1), (2, 0)), ((1, 1), (2, 1)))
 
 
 def _iota(shape, dim):
@@ -117,10 +116,8 @@
     has_above = lat > 0
     has_below = lat < n_lat - 1
     middle_band = n_lat // 2
-    relayed = n_lat >= 4 and n_lat % 2 == 0 and n_lon % 4 == 0
-    across = lon + 2 - 4 * (lon // 2 % 2) if relayed else lon
-    near_middle = [lat == middle_band - 1, lat == middle_band] if relayed else [False, False]
-    is_relay = [lat == 0, lat == n_lat - 1] if relayed else [False, False]
+    apart = n_lat >= 4
+    late_peer = lat == middle_band if apart else False
 
     def as_int(condition):
         return jnp.where(condition, 1, 0)
@@ -145,33 +142,27 @@
 
     greet(left)
     greet(right)
-    greets_below = has_below & jnp.logical_not(near_middle[0]) if relayed else has_below
+    greets_below = has_below
+    if apart:
+        greets_below = has_below & (lat != middle_band - 1)
     pl.when(has_above)(lambda: greet(above))
     pl.when(greets_below)(lambda: greet(below))
     peers = 2 + as_int(has_above) + as_int(has_below)
-    if relayed:
-        for place, partners in (
-            (is_relay[0], (middle_band - 1, middle_band)),
-            (is_relay[1], (middle_band - 1,)),
-            (near_middle[1], (n_lat - 1,)),
-        ):
-            for partner in partners:
-                pl.when(place)(functools.partial(greet, (partner, across)))
-        peers += 2 * as_int(near_middle[0]) + as_int(is_relay[1])
+    if apart:
+        peers -= as_int(late_peer)
     pl.semaphore_wait(barrier, peers)
-    if relayed:
-
-        @pl.when(near_middle[0])
+    if apart:
+
+        @pl.when(lat == middle_band - 1)
         def _():
-            for device in ((0, across), below):
-                pl.semaphore_signal(ready, inc=1, device_id=device, device_id_type=MESH)
-
-    def remote(src, dst, sems, index, device, landing=None):
+            pl.semaphore_signal(ready, inc=1, device_id=below, device_id_type=MESH)
+
+    def remote(src, dst, sems, index, device):
         return pltpu.make_async_remote_copy(
             src_ref=src,
             dst_ref=dst,
             send_sem=sems.at[(0,) + index],
-            recv_sem=sems.at[(1,) + (index if landing is None else landing)],
+            recv_sem=sems.at[(1,) + index],
             device_id=device,
             device_id_type=MESH,
         )
@@ -182,53 +173,18 @@
         src, dst = row_buffers[what]
         rows = pl.ds(13, 3) if side == 0 else pl.ds(0, 3)
         strips = pl.ds(chunk * width, width)
-        device, slot = (below, above)[side], side
-        if relayed:
-            turn = as_int(near_middle[side])
-            hop = middle_band - 1 if side == 1 else n_lat - 1 - middle_band
-            direction = 1 - 2 * side
-            device = (
-                lat + direction * (1 + turn * hop),
-                lon + turn * (across - lon),
-            )
-            slot = side + direction * turn
         return remote(
             src.at[rows, strips],
-            dst.at[slot, pl.ds(0, 3), strips],
+            dst.at[side, pl.ds(0, 3), strips],
             row_sems,
             (what, chunk, side),
-            device,
-            (what, chunk, slot),
-        )
-
-    def row_forward(what, chunk, side):
-        buffer = row_buffers[what][1]
-        strips = pl.ds(chunk * width, width)
-        return remote(
-            buffer.at[side, pl.ds(0, 3), strips],
-            buffer.at[1 - side, pl.ds(0, 3), strips],
-            row_sems,
-            (what, chunk, 1 - side),
-            (middle_band - 1 + side, across),
+            (below, above)[side],
         )
 
     def await_rows(what, chunk, side):
         buffer = row_buffers[what][1]
         rows = buffer.at[side, pl.ds(0, 3), pl.ds(chunk * width, width)]
         remote(rows, rows, row_sems, (what, chunk, side), left).wait_recv()
-
-    def forward(pieces, first=False):
-        if not relayed:
-            return
-        for side in range(2):
-
-            @pl.when(is_relay[side])
-            def _():
-                if first and side == 0:
-                    pl.semaphore_wait(ready, 1)
-                for what, chunk in pieces:
-                    await_rows(what, chunk, side)
-                    row_forward(what, chunk, side).start()
 
     def rim_copy(what, side):
         src = (k_hbm, v_hbm)[what]
@@ -250,12 +206,19 @@
             (lat - 1 + 2 * side, lon),
         )
 
-    def grad_copy(what, side):
+    def await_back(chunk, side):
+        part = dq_recv.at[side, :, pl.ds(chunk * width, width)]
+        remote(part, part, back_sems, (chunk, side), left).wait_recv()
+
+    rim_parts = ((2, 4), (0, 2), (6, 2))
+
+    def grad_copy(what, side, part):
+        pairs = pl.ds(*rim_parts[part])
         return remote(
-            rim_send.at[side, what],
-            rim_recv.at[side, what],
+            rim_send.at[side, what, pairs],
+            rim_recv.at[side, what, pairs],
             grad_sems,
-            (what, side),
+            (what, side, part),
             right if side == 0 else left,
         )
 
@@ -267,14 +230,13 @@
                 row_copy(what, chunk, side).start()
 
     every = range(CHUNKS)
-    for side in range(2):
-        if relayed:
-            pl.when(near_middle[side])(functools.partial(send_rows, (0, 1), side, every))
+    if apart:
+        pl.when(lat == middle_band - 1)(functools.partial(send_rows, (0, 1), 0, every))
     for chunk in every:
         for side in range(2):
             first = has[1 - side]
-            if relayed:
-                first = first & jnp.logical_not(near_middle[side])
+            if apart:
+                first = first & (lat != middle_band - 1 + side)
             pl.when(first)(functools.partial(send_rows, (0, 1), side, (chunk,)))
     for what in range(2):
         for side in range(2):
@@ -330,7 +292,8 @@
     pl.when(has_below)(lambda: send_rows((2,), 0, every))
     for r in (0, 1, 2):
         features_of(r)
-    pl.when(has_above)(lambda: send_rows((2,), 1, every))
+    early = has_above & jnp.logical_not(late_peer) if apart else has_above
+    pl.when(early)(lambda: send_rows((2,), 1, every))
     for r in range(3, 13):
         features_of(r)
 
@@ -429,9 +392,14 @@
         pipelined(todo, front, middle, back, use)
 
     strips([1, 2])
-    forward(RELAY_STEPS[0], True)
+    if apart:
+
+        @pl.when(late_peer)
+        def _():
+            pl.semaphore_wait(ready, 1)
+            send_rows((0, 1, 2), 1, every)
+
     strips([3, 4])
-    forward(RELAY_STEPS[1])
 
     for what in range(2):
         for side in range(2):
@@ -441,7 +409,27 @@
         dst[8] = jnp.where(half, turned(src[:, 7]), turned(rim_in[1, i])).astype(BF)
 
     strips([0, 7])
-    forward(RELAY_STEPS[2])
+
+    half8 = _iota((8, 512), 0) < 4
+
+    def send_rims(parts):
+        for what, acc in enumerate((dk_acc, dv_acc)):
+            scale = 0.125 if what == 0 else 1.0
+            for part in parts:
+                start, count = rim_parts[part]
+                for i in range(start, start + count):
+                    a, b = acc[8, 2 * i], acc[8, 2 * i + 1]
+                    rim_send[0, what, i] = (
+                        jnp.where(half8, pltpu.roll(a, 4, 0), b) * scale
+                    ).astype(BF)
+                    a, b = acc[0, 2 * i], acc[0, 2 * i + 1]
+                    rim_send[1, what, i] = (
+                        jnp.where(half8, a, pltpu.roll(b, 4, 0)) * scale
+                    ).astype(BF)
+                for side in range(2):
+                    grad_copy(what, side, part).start()
+
+    send_rims((0,))
 
     prob_halo = _prob_features(96)
 
@@ -496,12 +484,10 @@
     @pl.loop(0, 2 * CHUNKS)
     def _(k):
         chunk, side = k // 2, k % 2
-        if relayed:
-            middle_one = as_int(near_middle[0] | near_middle[1])
-            chunk = chunk + middle_one * (k % CHUNKS - chunk)
-            side = side + middle_one * (k // CHUNKS - side)
-            turn = as_int(near_middle[1])
-            side = side + turn * (1 - 2 * side)
+        if apart:
+            turn = as_int(late_peer)
+            chunk = chunk + turn * (k % CHUNKS - chunk)
+            side = side + turn * (1 - k // CHUNKS - side)
 
         @pl.when(has_above & (side == 0) | has_below & (side == 1))
         def _():
@@ -509,28 +495,9 @@
                 await_rows(what, chunk, side)
             todo = [(chunk * width + 2 * i, side, p) for i in range(width // 2) for p in range(4)]
             pipelined(todo, halo_front, halo_middle, halo_back, lambda j, done: None)
-            if relayed:
-
-                @pl.when(near_middle[1] & (side == 0) & (chunk == 0))
-                def _():
-                    pl.semaphore_wait(ready, 1)
-
             back_copy(chunk, side).start()
 
-    half8 = _iota((1, 8, 512), 1) < 4
-    for what, acc in enumerate((dk_acc, dv_acc)):
-        scale = 0.125 if what == 0 else 1.0
-        for i in range(8):
-            a, b = acc[8, 2 * i], acc[8, 2 * i + 1]
-            rim_send[0, what, i] = (
-                jnp.where(half8[0], pltpu.roll(a, 4, 0), b) * scale
-            ).astype(BF)
-            a, b = acc[0, 2 * i], acc[0, 2 * i + 1]
-            rim_send[1, what, i] = (
-                jnp.where(half8[0], a, pltpu.roll(b, 4, 0)) * scale
-            ).astype(BF)
-        for side in range(2):
-            grad_copy(what, side).start()
+    send_rims((1, 2))
 
     strips([5, 6])
 
@@ -548,29 +515,30 @@
 
     for what in range(2):
         for side in range(2):
-            grad_copy(what, side).wait()
+            for part in range(3):
+                grad_copy(what, side, part).wait()
     for what, (acc, out) in enumerate(((dk_acc, dk_out), (dv_acc, dv_out))):
         scale = 0.125 if what == 0 else 1.0
         edge = merged(acc, 0, scale)
         came = rim_recv[0, what].astype(F32)
         spun = pltpu.roll(came, 4, 1)
         for i in range(8):
-            out[2 * i, 0] = (edge[2 * i] + _keep(half8[0], came[i])).astype(BF)
-            out[2 * i + 1, 0] = (edge[2 * i + 1] + _keep(half8[0], spun[i])).astype(BF)
+            out[2 * i, 0] = (edge[2 * i] + _keep(half8, came[i])).astype(BF)
+            out[2 * i + 1, 0] = (edge[2 * i + 1] + _keep(half8, spun[i])).astype(BF)
         edge = merged(acc, 7, scale)
         came = rim_recv[1, what].astype(F32)
         spun = pltpu.roll(came, 4, 1)
         for i in range(8):
-            out[2 * i, 7] = (edge[2 * i] + _keep(jnp.logical_not(half8[0]), spun[i])).astype(BF)
+            out[2 * i, 7] = (edge[2 * i] + _keep(jnp.logical_not(half8), spun[i])).astype(BF)
             out[2 * i + 1, 7] = (
-                edge[2 * i + 1] + _keep(jnp.logical_not(half8[0]), came[i])
+                edge[2 * i + 1] + _keep(jnp.logical_not(half8), came[i])
             ).astype(BF)
 
     def finish(side, rows):
         @pl.when(has_above if side == 0 else has_below)
         def _():
             for chunk in range(CHUNKS):
-                back_copy(chunk, 1 - side).wait_recv()
+                await_back(chunk, side)
             for r in range(3):
                 dq_out[rows + r] = (
                     dq_acc[rows + r] * 0.125 + dq_recv[side, r].astype(F32)
@@ -589,15 +557,6 @@
             for what in range(3):
                 row_copy(what, chunk, send_side).wait_send()
             back_copy(chunk, back_side).wait_send()
-
-    if relayed:
-        for side in range(2):
-
-            @pl.when(is_relay[side])
-            def _():
-                for pieces in RELAY_STEPS:
-                    for what, chunk in pieces:
-                        row_forward(what, chunk, side).wait_send()
 
     pl.when(has_below)(lambda: drain(0, 1))
     pl.when(has_above)(lambda: drain(1, 0))
@@ -656,7 +615,7 @@
                 dma((2, 2, 2)),
                 dma((2, 3, CHUNKS, 2)),
                 dma((2, CHUNKS, 2)),
-                dma((2, 2, 2)),
+                dma((2, 2, 2, 3)),
                 pltpu.SemaphoreType.REGULAR,
             ],
             compiler_params=pltpu.CompilerParams(

time: 33.8 us -> 31.9 us (0.944)
  the two profiles are of different devices: /device:TPU:25 before, /device:TPU:22 now
where the time goes in v5:
time: 31.9 us; the launch traced here: 31.7 us
  Pallas kernels  31.1 us (97%)
  between operations  0.64 us (2%)
    pallas_call x1, Pallas kernels, per_device(): pl.pallas_call(functools.partial(kernel, n_lat, n_lon), out_shape=[pltpu....  29.4 us
    pallas_call x1, Pallas kernels, per_device(): pl.pallas_call(store_kernel, out_shape=[jax.ShapeDtypeStruct(token, BF)]...  1.69 us

profile of v5, /device:TPU:22, one launch (start us, length us, event | category | flops | bytes accessed | tf_op | source)
XLA Modules:
  0.0 31.7 jit_solution(9143088814457565827)
XLA Ops:
  0.6 29.4 %shard_map.85 = (bf16[16,8,8,512]{3,2,1,0:T(8,128)(2,1)S(1)}, bf16[16,8,8,512]{3,2,1,0:T(8,128)(2,1)S(1)}, bf16[16,8,8,512]{3,2,1,0:T(8,128)(2,1)S(1)}) custom-call(bf16[16,8,8,512]{3,2,1,0:T(8,128)(2,1)} %bitcast.9, bf16[16,8,8,512]{3,2,1,0:T(8,128)(2,1)} %bitcast.10, bf16[16,8,8,512]{3,2,1,0:T(8,128)(2,1)} %bitcast.11, bf16[16,8,8,512]{3,2,1,0:T(8,128)(2,1)} %bitcast.12, ...), custom_call_target="tpu_custom_call" | custom-call | tf_op jit(solution)/shard_map/pallas_call | solution.py:586
  30.0 1.7 %shard_map.86 = (bf16[16,8,8,512]{3,2,1,0:T(8,128)(2,1)}, bf16[16,8,8,512]{3,2,1,0:T(8,128)(2,1)}, bf16[16,8,8,512]{3,2,1,0:T(8,128)(2,1)}) custom-call(bf16[16,8,8,512]{3,2,1,0:T(8,128)(2,1)S(1)} %get-tuple-element.9.a, bf16[16,8,8,512]{3,2,1,0:T(8,128)(2,1)S(1)} %get-tuple-element.10.b, bf16[16,8,8,512]{3,2,1,0:T(8,128)(2,1)S(1)} %get-tuple-element.11.c), custom_call_target="tpu_custom_call" | custom-call | tf_op jit(solution)/shard_map/pallas_call | solution.py:634

commit v6 on v5

--- a/solution.py
+++ b/solution.py
@@ -231,7 +231,7 @@
 
     every = range(CHUNKS)
     if apart:
-        pl.when(lat == middle_band - 1)(functools.partial(send_rows, (0, 1), 0, every))
+        pl.when(lat == middle_band - 1)(functools.partial(send_rows, (0, 1), 0, every[:1]))
     for chunk in every:
         for side in range(2):
             first = has[1 - side]
@@ -296,6 +296,8 @@
     pl.when(early)(lambda: send_rows((2,), 1, every))
     for r in range(3, 13):
         features_of(r)
+    if apart:
+        pl.when(lat == middle_band - 1)(functools.partial(send_rows, (0, 1), 0, every[1:]))
 
     half = _iota((1, 8, 512), 1) < 4
 
@@ -391,7 +393,6 @@
 
         pipelined(todo, front, middle, back, use)
 
-    strips([1, 2])
     if apart:
 
         @pl.when(late_peer)
@@ -399,6 +400,7 @@
             pl.semaphore_wait(ready, 1)
             send_rows((0, 1, 2), 1, every)
 
+    strips([1, 2])
     strips([3, 4])
 
     for what in range(2):

time: 31.9 us -> 32.9 us (1.031)
  Pallas kernels: 31.1 us -> 32.2 us
    pallas_call x1, Pallas kernels: 29.4 us -> 30.5 us  [per_device(): pl.pallas_call(functools.partial(kernel, n_lat, n_lon), out_shape=[pltpu....]
where the time goes in v6:
time: 32.9 us; the launch traced here: 32.8 us
  Pallas kernels  32.2 us (98%)
  between operations  0.64 us (2%)
    pallas_call x1, Pallas kernels, per_device(): pl.pallas_call(functools.partial(kernel, n_lat, n_lon), out_shape=[pltpu....  30.5 us
    pallas_call x1, Pallas kernels, per_device(): pl.pallas_call(store_kernel, out_shape=[jax.ShapeDtypeStruct(token, BF)]...  1.69 us

profile of v6, /device:TPU:22, one launch (start us, length us, event | category | flops | bytes accessed | tf_op | source)
XLA Modules:
  0.0 32.8 jit_solution(14532408994538902766)
XLA Ops:
  0.6 30.5 %shard_map.85 = (bf16[16,8,8,512]{3,2,1,0:T(8,128)(2,1)S(1)}, bf16[16,8,8,512]{3,2,1,0:T(8,128)(2,1)S(1)}, bf16[16,8,8,512]{3,2,1,0:T(8,128)(2,1)S(1)}) custom-call(bf16[16,8,8,512]{3,2,1,0:T(8,128)(2,1)} %bitcast.9, bf16[16,8,8,512]{3,2,1,0:T(8,128)(2,1)} %bitcast.10, bf16[16,8,8,512]{3,2,1,0:T(8,128)(2,1)} %bitcast.11, bf16[16,8,8,512]{3,2,1,0:T(8,128)(2,1)} %bitcast.12, ...), custom_call_target="tpu_custom_call" | custom-call | tf_op jit(solution)/shard_map/pallas_call | solution.py:588
  31.1 1.7 %shard_map.86 = (bf16[16,8,8,512]{3,2,1,0:T(8,128)(2,1)}, bf16[16,8,8,512]{3,2,1,0:T(8,128)(2,1)}, bf16[16,8,8,512]{3,2,1,0:T(8,128)(2,1)}) custom-call(bf16[16,8,8,512]{3,2,1,0:T(8,128)(2,1)S(1)} %get-tuple-element.9.a, bf16[16,8,8,512]{3,2,1,0:T(8,128)(2,1)S(1)} %get-tuple-element.10.b, bf16[16,8,8,512]{3,2,1,0:T(8,128)(2,1)S(1)} %get-tuple-element.11.c), custom_call_target="tpu_custom_call" | custom-call | tf_op jit(solution)/shard_map/pallas_call | solution.py:636
